TPU v7x, 32 devices: a whole 2x2x4 slice. The times are simulated.
32 devices in a mesh: section: 2 (over core), dp: 16 (over z, y, x).
Axes of the slice: x: 2, y: 2, z: 4, core: 2. Of those that a mesh axis runs over, the one named last changes fastest.
Arguments:
- inputs: bfloat16 [2, 16, 256, 768], P(None, 'dp'), may hold values from -6 to 6
- cotangent: bfloat16 [2, 16, 256, 768], P(None, 'dp'), may hold values from -6 to 6
- lengths: int32 [2, 16], P(None, 'dp'), may hold values from 64 to 256, as said below
- w_query: bfloat16 [2, 768, 768], P('section'), may hold values from -0.21875 to 0.21875
- w_key: bfloat16 [2, 768, 768], P('section'), may hold values from -0.21875 to 0.21875
- w_value: bfloat16 [2, 768, 768], P('section'), may hold values from -0.21875 to 0.21875
- w_output: bfloat16 [2, 768, 768], P('section'), may hold values from -1.75 to 1.75
- w_in: bfloat16 [2, 768, 3072], P('section'), may hold values from -0.21875 to 0.21875
- w_out: bfloat16 [2, 3072, 768], P('section'), may hold values from -0.109375 to 0.109375
- gain_attn: float32 [2, 768], P('section'), may hold values from 0.5 to 1.5
- gain_ffn: float32 [2, 768], P('section'), may hold values from 0.5 to 1.5
- mix_pre: float32 [2, 12, 12], P('section'), may hold values from -1.75 to 1.75
- mix_post: float32 [2, 12, 12], P('section'), may hold values from -1.75 to 1.75
Outputs:
- layer_outputs: bfloat16 [2, 2, 16, 256, 768], P('section', None, 'dp')
- input_grads: bfloat16 [2, 2, 16, 256, 768], P('section', None, 'dp')
- grad_query: float32 [2, 768, 768], P('section')
- grad_key: float32 [2, 768, 768], P('section')
- grad_value: float32 [2, 768, 768], P('section')
- grad_output: float32 [2, 768, 768], P('section')
- grad_in: float32 [2, 768, 3072], P('section')
- grad_out: float32 [2, 3072, 768], P('section')
- grad_gain_attn: float32 [2, 768], P('section')
- grad_gain_ffn: float32 [2, 768], P('section')
- grad_mix_pre: float32 [2, 12, 12], P('section')
- grad_mix_post: float32 [2, 12, 12], P('section')
- rms_stats: float32 [2, 3], P('section')
Inputs may be any that keep to these rules, and one draw needn't show every extreme that they name: Sequence s of micro-batch m holds valid tokens at positions 0 to lengths[m, s] - 1 of its padded row; some sequence has length 256 and some has length 64.
All inputs are finite; a program needn't handle non-finite values.
Results may differ from a plain program's by a relative error of at most 0.018.
Values may be sent and summed in bfloat16 or wider, within the bound.
No kernel may reach another device: no remote copies, remote signals or barrier semaphores. Data moves between devices by JAX's collectives and lax.ppermute only.
A program may use at most 256 MiB of HBM per device.

v0:
```python
import jax
import jax.numpy as jnp
from jax import lax
from jax.sharding import PartitionSpec as P

EPSILON = 1e-06
MASKED = -1e30
HIGHEST = lax.Precision.HIGHEST


def shifted_2(shard, axis, by):
    length = lax.axis_size(axis)
    pairs = [(i, i + by) for i in range(length) if 0 <= i + by < length]
    return lax.ppermute(shard, axis, pairs)


def norm_part(values, gain):
    return values * lax.rsqrt(jnp.mean(values * values, axis=-1, keepdims=True) + EPSILON) * gain


def gelu_tanh(values):
    return (
        0.5
        * values
        * (1.0 + jnp.tanh(0.7978845608028654 * (values + 0.044715 * values * values * values)))
    )


def talking(scores, mix_pre, mix_post):
    length = scores.shape[-1]
    rows = lax.broadcasted_iota(jnp.int32, (length, length), 0)
    columns = lax.broadcasted_iota(jnp.int32, (length, length), 1)
    logits = jnp.einsum("gh,...hij->...gij", mix_pre, scores, precision=HIGHEST)
    logits = jnp.where(columns <= rows, logits, MASKED)
    shifted = logits - jnp.max(logits, axis=-1, keepdims=True)
    exponent = jnp.exp(shifted)
    normalized = exponent / jnp.sum(exponent, axis=-1, keepdims=True)
    return jnp.einsum("gh,...hij->...gij", mix_post, normalized, precision=HIGHEST)


def project(values, weight):
    return jnp.einsum("spd,dc->spc", values, weight, preferred_element_type=jnp.float32)


def unchanged(group):
    return group


def layer_forward(values, valid, params):
    w_query, w_key, w_value, w_output, w_in, w_out, gain_attn, gain_ffn, mix_pre, mix_post = params
    seq_count, length, width = values.shape
    head_count = mix_pre.shape[0]
    head_dim = width // head_count
    split = (seq_count, length, head_count, head_dim)
    normed = norm_part(values, gain_attn).astype(jnp.bfloat16)
    query = project(normed, w_query).astype(jnp.bfloat16).reshape(split)
    key_rows = project(normed, w_key).astype(jnp.bfloat16).reshape(split)
    value_rows = project(normed, w_value).astype(jnp.bfloat16).reshape(split)
    scores = jnp.einsum(
        "sihd,sjhd->shij", query, key_rows, preferred_element_type=jnp.float32
    ) * head_dim ** (-0.5)
    attn_weights = talking(scores, mix_pre, mix_post).astype(jnp.bfloat16)
    head_out = jnp.einsum(
        "shij,sjhd->sihd", attn_weights, value_rows, preferred_element_type=jnp.float32
    )
    head_out = head_out.astype(jnp.bfloat16).reshape(seq_count, length, width)
    branch_attn = project(head_out, w_output)
    residual = values + branch_attn
    normed_ffn = norm_part(residual, gain_ffn).astype(jnp.bfloat16)
    pre_act = project(normed_ffn, w_in)
    activation = gelu_tanh(pre_act).astype(jnp.bfloat16)
    branch_ffn = project(activation, w_out)
    layer_out = valid[..., None] * (residual + branch_ffn)
    sums = jnp.stack(
        [
            jnp.sum(jnp.mean(layer_out * layer_out, axis=-1)),
            jnp.sum(valid * jnp.mean(branch_attn * branch_attn, axis=-1)),
            jnp.sum(valid * jnp.mean(branch_ffn * branch_ffn, axis=-1)),
        ]
    )
    saved = (
        normed,
        query,
        key_rows,
        value_rows,
        scores,
        attn_weights,
        head_out,
        residual,
        normed_ffn,
        pre_act,
        activation,
    )
    return (layer_out, sums, saved)


def layer_backward(values, valid, params, upstream, prior, hooks):
    w_query, w_key, w_value, w_output, w_in, w_out, gain_attn, gain_ffn, mix_pre, mix_post = params
    layer_out, sums, saved = layer_forward(values, valid, params)
    (
        normed,
        query,
        key_rows,
        value_rows,
        scores,
        attn_weights,
        head_out,
        residual,
        normed_ffn,
        pre_act,
        activation,
    ) = saved
    seq_count, length, width = values.shape
    head_count = mix_pre.shape[0]
    head_dim = width // head_count
    split = (seq_count, length, head_count, head_dim)
    grad_sum = valid[..., None] * upstream
    grad_branch = grad_sum.astype(jnp.bfloat16)
    grad_down = jnp.einsum(
        "spf,spd->fd", activation, grad_branch, preferred_element_type=jnp.float32
    )
    grad_act = jnp.einsum("spd,fd->spf", grad_branch, w_out, preferred_element_type=jnp.float32)
    gelu_back = jax.vjp(gelu_tanh, pre_act)[1]
    grad_pre = gelu_back(grad_act)[0].astype(jnp.bfloat16)
    grad_up = jnp.einsum("spd,spf->df", normed_ffn, grad_pre, preferred_element_type=jnp.float32)
    ffn_done = hooks[0]((prior[4] + grad_up.reshape(-1), prior[5] + grad_down.reshape(-1)))
    grad_normed_ffn = jnp.einsum("spf,df->spd", grad_pre, w_in, preferred_element_type=jnp.float32)
    second_norm_back = jax.vjp(norm_part, residual, gain_ffn)[1]
    grad_resid_norm, grad_gain_ffn = second_norm_back(grad_normed_ffn)
    grad_resid = grad_sum + grad_resid_norm
    grad_attn = grad_resid.astype(jnp.bfloat16)
    grad_proj = jnp.einsum("spc,spd->cd", head_out, grad_attn, preferred_element_type=jnp.float32)
    proj_done = hooks[1]((prior[3] + grad_proj.reshape(-1),))
    grad_heads = jnp.einsum("spd,cd->spc", grad_attn, w_output, preferred_element_type=jnp.float32)
    grad_heads = grad_heads.astype(jnp.bfloat16).reshape(split)
    grad_weights = jnp.einsum(
        "sihd,sjhd->shij", grad_heads, value_rows, preferred_element_type=jnp.float32
    )
    grad_value_rows = jnp.einsum(
        "shij,sihd->sjhd", attn_weights, grad_heads, preferred_element_type=jnp.float32
    )
    grad_value_rows = grad_value_rows.astype(jnp.bfloat16).reshape(seq_count, length, width)
    talk_back = jax.vjp(talking, scores, mix_pre, mix_post)[1]
    grad_scores, grad_mix_pre, grad_mix_post = talk_back(grad_weights)
    grad_scores = grad_scores.astype(jnp.bfloat16)
    scale = head_dim ** (-0.5)
    grad_queries = (
        jnp.einsum("shij,sjhd->sihd", grad_scores, key_rows, preferred_element_type=jnp.float32)
        * scale
    )
    grad_queries = grad_queries.astype(jnp.bfloat16).reshape(seq_count, length, width)
    grad_keys = (
        jnp.einsum("shij,sihd->sjhd", grad_scores, query, preferred_element_type=jnp.float32)
        * scale
    )
    grad_keys = grad_keys.astype(jnp.bfloat16).reshape(seq_count, length, width)
    pieces = (grad_queries, grad_keys, grad_value_rows)
    matrices = (w_query, w_key, w_value)
    projection_grads = tuple(
        (
            jnp.einsum("spd,spc->dc", normed, piece, preferred_element_type=jnp.float32)
            for piece in pieces
        )
    )
    qkv_done = hooks[2](
        (
            prior[0] + projection_grads[0].reshape(-1),
            prior[1] + projection_grads[1].reshape(-1),
            prior[2] + projection_grads[2].reshape(-1),
        )
    )
    grad_normed = sum(
        (
            jnp.einsum("spc,dc->spd", piece, matrix, preferred_element_type=jnp.float32)
            for piece, matrix in zip(pieces, matrices)
        )
    )
    first_norm_back = jax.vjp(norm_part, values, gain_attn)[1]
    grad_in_norm, grad_gain_attn = first_norm_back(grad_normed)
    grad_input = grad_resid + grad_in_norm
    big = (qkv_done[0], qkv_done[1], qkv_done[2], proj_done[0], ffn_done[0], ffn_done[1])
    small = (grad_gain_attn, grad_gain_ffn, grad_mix_pre, grad_mix_post)
    return (grad_input, big, small)


def local(
    inputs,
    cotangent,
    lengths,
    w_query,
    w_key,
    w_value,
    w_output,
    w_in,
    w_out,
    gain_attn,
    gain_ffn,
    mix_pre,
    mix_post,
):
    is_first = lax.axis_index("section") == 0
    params = (
        w_query[0],
        w_key[0],
        w_value[0],
        w_output[0],
        w_in[0],
        w_out[0],
        gain_attn[0],
        gain_ffn[0],
        mix_pre[0],
        mix_post[0],
    )
    blocks, seq_count, length, width = inputs.shape
    valid = (
        lax.broadcasted_iota(jnp.int32, (blocks, seq_count, length), 2) < lengths[:, :, None]
    ).astype(jnp.float32)
    received = []
    outputs = []
    square_sums = jnp.zeros((3,), jnp.float32)
    for moment in range(blocks + 1):
        early = min(moment, blocks - 1)
        later = max(moment - 1, 0)
        own_input = inputs[early]
        if moment > 0:
            layer_in = jnp.where(is_first, own_input, received[later])
        else:
            layer_in = own_input
        row_valid = jnp.where(is_first, valid[early], valid[later])
        active = jnp.where(is_first, moment < blocks, moment >= 1)
        layer_out, sums, saved = layer_forward(layer_in.astype(jnp.float32), row_valid, params)
        square_sums = square_sums + jnp.where(active, sums, 0.0)
        rounded = layer_out.astype(jnp.bfloat16)
        if moment < blocks:
            received.append(shifted_2(rounded, "section", 1))
        outputs.append(rounded)
    big_acc = tuple((jnp.zeros((weight.size,), jnp.float32) for weight in params[:6]))
    small_acc = tuple((jnp.zeros(weight.shape, jnp.float32) for weight in params[6:]))
    plain = (unchanged, unchanged, unchanged)
    sent = None
    grad_list = []
    for moment in range(blocks + 1):
        later = min(moment, blocks - 1)
        early = max(moment - 1, 0)
        layer_in = jnp.where(is_first, inputs[early], received[later])
        row_valid = jnp.where(is_first, valid[early], valid[later])
        active = jnp.where(is_first, moment >= 1, moment < blocks)
        upstream = cotangent[later].astype(jnp.float32)
        if sent is not None:
            upstream = jnp.where(is_first, sent.astype(jnp.float32), upstream)
        upstream = jnp.where(active, upstream, 0.0)
        grad_input, big_acc, small = layer_backward(
            layer_in.astype(jnp.float32), row_valid, params, upstream, big_acc, plain
        )
        small_acc = tuple((total + grad for total, grad in zip(small_acc, small)))
        grad_rounded = grad_input.astype(jnp.bfloat16)
        if moment < blocks:
            sent = shifted_2(grad_rounded, "section", -1)
        grad_list.append(grad_rounded)
    big_acc = lax.psum_scatter(big_acc, "dp", scatter_dimension=0, tiled=True)
    whole = lax.all_gather(big_acc, "dp", axis=0, tiled=True)
    count = jnp.sum(valid)
    totals = lax.psum(
        (small_acc[0], small_acc[1], small_acc[2], small_acc[3], square_sums, count), "dp"
    )
    rms = jnp.sqrt(totals[4] / totals[5])[None]
    layer_outputs = jnp.stack(
        [
            jnp.where(is_first, outputs[block_index], outputs[block_index + 1])
            for block_index in range(blocks)
        ]
    )[None]
    input_grads = jnp.stack(
        [
            jnp.where(is_first, grad_list[block_index + 1], grad_list[block_index])
            for block_index in range(blocks)
        ]
    )[None]
    big_grads = tuple((flat.reshape(weight.shape)[None] for flat, weight in zip(whole, params[:6])))
    return (
        layer_outputs,
        input_grads,
        big_grads[0],
        big_grads[1],
        big_grads[2],
        big_grads[3],
        big_grads[4],
        big_grads[5],
        totals[0][None],
        totals[1][None],
        totals[2][None],
        totals[3][None],
        rms,
    )


def solution(mesh):
    in_specs = (
        P(None, "dp", None, None),
        P(None, "dp", None, None),
        P(None, "dp"),
        P("section", None, None),
        P("section", None, None),
        P("section", None, None),
        P("section", None, None),
        P("section", None, None),
        P("section", None, None),
        P("section", None),
        P("section", None),
        P("section", None, None),
        P("section", None, None),
    )
    out_specs = (
        P("section", None, "dp", None, None),
        P("section", None, "dp", None, None),
        P("section", None, None),
        P("section", None, None),
        P("section", None, None),
        P("section", None, None),
        P("section", None, None),
        P("section", None, None),
        P("section", None),
        P("section", None),
        P("section", None, None),
        P("section", None, None),
        P("section", None),
    )
    return jax.shard_map(local, mesh=mesh, in_specs=in_specs, out_specs=out_specs, check_vma=False)
```

profile of v0, /device:TPU:0, one launch (start us, length us, event | category | flops | bytes accessed | tf_op | source)
XLA Modules:
  0.0 1703.9 jit_solution(4690759240372660346)
XLA Ops:
  20.8 7.1 bitcast_reduce_fusion.4
  37.3 8.0 multiply_reduce_fusion.8
  62.3 7.1 bitcast_reduce_fusion.1
  85.4 6.8 fusion.102
  109.0 10.8 fusion.65
  122.1 12.5 fusion.88
  176.9 8.2 multiply_reduce_fusion.3
  203.3 7.1 bitcast_reduce_fusion
  213.2 6.0 convert_bitcast_fusion.2
  226.5 6.9 fusion.106
  248.5 11.0 fusion.57
  262.9 11.8 fusion.89
  318.0 7.2 fusion.152
  341.7 8.2 fusion.53
  350.0 8.0 fusion.90
  395.9 13.5 add_add_fusion
  409.4 10.7 add.403
  420.2 8.4 add_bitcast_fusion
  436.3 741.0 %all-reduce.10.cloned.1.call-done = (f32[589824]{0:T(1024)}, f32[589824]{0:T(1024)}, f32[589824]{0:T(1024)}, f32[589824]{0:T(1024)}, f32[2359296]{0:T(1024)}, /*index=5*/f32[2359296]{0:T(1024)}) async-done(((f32[589824]{0:T(1024)}, f32[589824]{0:T(1024)}, f32[589824]{0:T(1024)}, f32[589824]{0:T(1024)}, f32[2359296]{0:T(1024)}, /*index=5*/f32[2359296]{0:T(1024)}), (f32[589824]{0:T(1024)}, f32[589824]{0:T(1024)}, ...) | async-done | bytes 28311568
  1193.9 9.5 fusion.230
  1203.4 6.9 fusion.236
  1212.7 7.3 fusion.261
  1229.7 6.4 fusion.227
  1236.1 6.5 fusion.272
  1242.7 7.5 fusion.256
  1250.2 75.3 %all-reduce.6 = (f32[1,768]{1,0:T(1,128)}, f32[1,768]{1,0:T(1,128)}, f32[1,12,12]{2,1,0:T(8,128)S(1)}, f32[1,12,12]{2,1,0:T(8,128)S(1)}, f32[3]{0:T(128)S(1)}, /*index=5*/f32[]{:T(128)}) all-reduce(f32[1,768]{1,0:T(1,128)S(1)} %broadcast_in_dim.207, ...), channel_id=1, replica_groups=mesh['section'=2,'dp'=16] {'dp'}, use_global_device_ids=true, to_apply=%region_44.45 | all-reduce | flops 1828 | bytes 14624 | tf_op jit(solution)/shard_map/psum | solution.py:263
  1337.0 35.3 %all-gather.13.cloned.1.call-done = f32[589824]{0:T(1024)} async-done(((f32[36864]{0:T(1024)}), f32[589824]{0:T(1024)}) %all-gather.13.cloned.1.call-update) | async-done | bytes 2359312 | tf_op jit(solution)/shard_map/all_gather | solution.py:261
  1375.6 60.8 %all-gather.11.cloned.1.call-done = f32[589824]{0:T(1024)} async-done(((f32[36864]{0:T(1024)}), f32[589824]{0:T(1024)}) %all-gather.11.cloned.1.call-update) | async-done | bytes 2359312 | tf_op jit(solution)/shard_map/all_gather | solution.py:261
  1439.8 121.6 %all-gather.17.cloned.1.call-done = f32[2359296]{0:T(1024)} async-done(((f32[147456]{0:T(1024)}), f32[2359296]{0:T(1024)}) %all-gather.17.cloned.1.call-update) | async-done | bytes 9437200 | tf_op jit(solution)/shard_map/all_gather | solution.py:261
  1561.3 11.3 broadcast_in_dim_reshape.23
  1572.6 113.1 %all-gather.15.cloned.1.call-done = f32[2359296]{0:T(1024)} async-done(((f32[147456]{0:T(1024)}), f32[2359296]{0:T(1024)}) %all-gather.15.cloned.1.call-update) | async-done | bytes 9437200 | tf_op jit(solution)/shard_map/all_gather | solution.py:261
  1685.8 10.9 broadcast_in_dim_reshape.22
  (526 shorter events, 312.8 us)
Async XLA Ops:
  7.2 28.7 %copy-start = (bf16[1,768,768]{2,1,0:T(8,128)(2,1)S(1)}, bf16[1,768,768]{2,1,0:T(8,128)(2,1)}, u32[]{:S(2)}) copy-start(bf16[1,768,768]{2,1,0:T(8,128)(2,1)} %param.19) | copy-start | bytes 3538948
  7.2 1170.1 %all-reduce.10.cloned.1.call-start = ((), (), s32[]{:S(2)}) async-start(), calls=%async_computation.6 | async-start | bytes 56623104
  9.3 39.5 %copy-start.130 = (f32[1,1,256]{2,0,1:T(1,128)}, f32[1,1,256]{2,0,1:T(1,128)S(1)}, u32[]{:S(2)}) copy-start(f32[1,1,256]{2,0,1:T(1,128)S(1)} %get-tuple-element.134) | copy-start | bytes 3076
  45.3 3.8 collective-permute-start
  48.8 136.3 %copy-start.135 = (f32[256]{0:T(256)}, f32[256]{0:T(256)S(1)}, u32[]{:S(2)}) copy-start(f32[256]{0:T(256)S(1)} %get-tuple-element.133) | copy-start | bytes 3076
  50.8 134.3 %copy-start.58 = (bf16[1,256,768]{2,1,0:T(8,128)(2,1)}, bf16[1,256,768]{2,1,0:T(8,128)(2,1)S(1)}, u32[]{:S(2)}) copy-start(bf16[1,256,768]{2,1,0:T(8,128)(2,1)S(1)} %get-tuple-element.125) | copy-start | bytes 1179652
  69.4 65.2 %copy-start.78 = (f32[12,256]{0,1:T(8,128)}, f32[12,256]{0,1:T(8,128)S(1)}, u32[]{:S(2)}) copy-start(f32[12,256]{0,1:T(8,128)S(1)} %get-tuple-element.140) | copy-start | bytes 36868
  71.5 63.1 %copy-start.117 = (f32[12,256]{0,1:T(8,128)}, f32[12,256]{0,1:T(8,128)S(1)}, u32[]{:S(2)}) copy-start(f32[12,256]{0,1:T(8,128)S(1)} %fusion.463) | copy-start | bytes 36868
  170.3 14.9 copy-start.29
  187.5 6.3 collective-permute-start.1
  190.1 36.4 %collective-permute-start.2 = (bf16[1,256,768]{2,1,0:T(8,128)(2,1)S(1)}, bf16[1,256,768]{2,1,0:T(8,128)(2,1)}, u32[]{:S(2)}, u32[]{:S(2)}) collective-permute-start(bf16[1,256,768]{2,1,0:T(8,128)(2,1)S(1)} %fusion.302), channel_id=1, source_target_pairs={{16,0},{17,1},{18,2},{19,3},{20,4},{21,5},{22,6},{23,7},{24,8},{25... | collective-permute-start | bytes 1179656 | tf_op jit(solution)/shard_map/ppermute | solution.py:14
  241.1 52.5 %copy-start.67 = (bf16[12,64,256]{2,1,0:T(8,128)(2,1)}, bf16[12,64,256]{2,1,0:T(8,128)(2,1)S(1)}, u32[]{:S(2)}) copy-start(bf16[12,64,256]{2,1,0:T(8,128)(2,1)S(1)} %convolution_convert_fusion.2) | copy-start | bytes 1179652
  260.3 14.4 copy-start.20
  299.3 26.0 %copy-start.80 = (f32[12,256]{0,1:T(8,128)}, f32[12,256]{0,1:T(8,128)S(1)}, u32[]{:S(2)}) copy-start(f32[12,256]{0,1:T(8,128)S(1)} %fusion.460) | copy-start | bytes 36868
  311.8 16.1 collective-permute-start.3
  318.0 14.9 copy-start.122
  339.8 33.1 %copy-start.69 = (bf16[12,64,256]{2,1,0:T(8,128)(2,1)}, bf16[12,64,256]{2,1,0:T(8,128)(2,1)S(1)}, u32[]{:S(2)}) copy-start(bf16[12,64,256]{2,1,0:T(8,128)(2,1)S(1)} %convolution_convert_fusion) | copy-start | bytes 1179652
  434.5 754.5 %copy-start.144 = (s32[2,1]{0,1:T(1,128)S(1)}, s32[2,1]{0,1:T(1,128)}, u32[]{:S(2)}) copy-start(s32[2,1]{0,1:T(1,128)} %param.15) | copy-start | bytes 28
  434.5 755.2 %copy-start.142 = (f32[256]{0:T(256)S(1)}, f32[256]{0:T(256)}, u32[]{:S(2)}) copy-start(f32[256]{0:T(256)} %get-tuple-element.85) | copy-start | bytes 3076
  434.5 755.2 %copy-start.140 = (f32[256]{0:T(256)S(1)}, f32[256]{0:T(256)}, u32[]{:S(2)}) copy-start(f32[256]{0:T(256)} %get-tuple-element.84) | copy-start | bytes 3076
  434.5 755.2 %copy-start.141 = (f32[256]{0:T(256)S(1)}, f32[256]{0:T(256)}, u32[]{:S(2)}) copy-start(f32[256]{0:T(256)} %get-tuple-element.86) | copy-start | bytes 3076
  434.5 755.8 %copy-start.59 = (bf16[1,256,768]{2,1,0:T(8,128)(2,1)S(1)}, bf16[1,256,768]{2,1,0:T(8,128)(2,1)}, u32[]{:S(2)}) copy-start(bf16[1,256,768]{2,1,0:T(8,128)(2,1)} %copy-done.58) | copy-start | bytes 1179652
  434.5 755.8 %copy-start.136 = (f32[256]{0:T(256)S(1)}, f32[256]{0:T(256)}, u32[]{:S(2)}) copy-start(f32[256]{0:T(256)} %copy-done.135) | copy-start | bytes 3076
  434.5 895.7 %all-gather.7.cloned.1.call-start = ((), (), s32[]{:S(2)}) async-start(), calls=%async_computation | async-start | bytes 2506752 | tf_op jit(solution)/shard_map/all_gather | solution.py:261
  1178.9 154.7 %all-gather.9.cloned.1.call-start = ((), (), s32[]{:S(2)}) async-start(), calls=%async_computation.1 | async-start | bytes 2506752 | tf_op jit(solution)/shard_map/all_gather | solution.py:261
  1180.6 191.7 %all-gather.13.cloned.1.call-start = ((), (), s32[]{:S(2)}) async-start(), calls=%async_computation.3 | async-start | bytes 2506752 | tf_op jit(solution)/shard_map/all_gather | solution.py:261
  1182.2 254.2 %all-gather.11.cloned.1.call-start = ((), (), s32[]{:S(2)}) async-start(), calls=%async_computation.2 | async-start | bytes 2506752 | tf_op jit(solution)/shard_map/all_gather | solution.py:261
  1183.9 377.4 %all-gather.17.cloned.1.call-start = ((), (), s32[]{:S(2)}) async-start(), calls=%async_computation.5 | async-start | bytes 10027008 | tf_op jit(solution)/shard_map/all_gather | solution.py:261
  1186.6 499.2 %all-gather.15.cloned.1.call-start = ((), (), s32[]{:S(2)}) async-start(), calls=%async_computation.4 | async-start | bytes 10027008 | tf_op jit(solution)/shard_map/all_gather | solution.py:261
  1242.6 84.0 %copy-start.138 = (f32[256]{0:T(256)S(1)}, f32[256]{0:T(256)}, u32[]{:S(2)}) copy-start(f32[256]{0:T(256)} %copy-done.137) | copy-start | bytes 3076
  1242.6 84.0 %copy-start.36 = (f32[1,256,768]{2,1,0:T(8,128)S(1)}, f32[1,256,768]{2,1,0:T(8,128)}, u32[]{:S(2)}) copy-start(f32[1,256,768]{2,1,0:T(8,128)} %copy-done.34) | copy-start | bytes 2359300
  1242.6 85.5 %copy-start.93 = (bf16[1,1,256,768]{3,2,1,0:T(8,128)(2,1)S(1)}, bf16[1,1,256,768]{3,2,1,0:T(8,128)(2,1)}, u32[]{:S(2)}) copy-start(bf16[1,1,256,768]{3,2,1,0:T(8,128)(2,1)} %get-tuple-element.107) | copy-start | bytes 1179652
  (133 other events, 688.3 us)
Sparse Core Ops, SparseCore 0:
  434.6 742.6 all-reduce.9
  1181.1 61.3 all-gather.6
  1246.2 61.7 all-gather.8
  1311.0 61.1 all-gather.12
  1375.3 61.0 all-gather.10
  1440.0 121.2 all-gather.16
  1565.1 120.6 all-gather.14
where the time goes:
time: 1710 us; the launch traced here: 1700 us
  waiting for transfers between devices  1070 us (63%)
  matrix products  360 us (21%)
  local copies, waits for them, and re-layouts  108 us (6%)
  blocking collectives  75.3 us (4%)
  other arithmetic  60.6 us (4%)
  between operations  18.3 us (1%)
    unnamed x8, waiting for transfers between devices  741 us
    all_gather x6, waiting for transfers between devices, local(): whole = lax.all_gather(big_acc, 'dp', axis=0, tiled=True)  331 us
    dot_general x11, matrix products, talking(): jnp.einsum('gh,...hij->...gij', mix_post, normalized, precision=HIGHEST)  80 us
    dot_general x11, matrix products, talking(): logits = jnp.einsum('gh,...hij->...gij', mix_pre, scores, precision=HIGHEST)  80 us
    psum x1, blocking collectives, local(): lax.psum((small_acc[0], small_acc[1], small_acc[2], small_acc[3], square_...  75.3 us
    dot_general x26, matrix products, project(): jnp.einsum('spd,dc->spc', values, weight, preferred_element_type=jnp.floa...  53.4 us
    another operation x6, local copies, waits for them, and re-layouts, local(): flat.reshape(weight.shape)[None]  35.6 us
  transfers between devices with their start and end apart: 11, of which 6 were waited for; matrix products, arithmetic and copies ran while one was open for 9% of the time, Pallas kernels for 0%

commit v1 on v0

v1 whole, which is shorter than its diff:
```python
import jax
import jax.numpy as jnp
from jax import lax
from jax.sharding import PartitionSpec as P

EPSILON = 1e-06
MASKED = -1e30
F32 = jnp.float32
BF16 = jnp.bfloat16


def dot(a, b, dims):
    return lax.dot_general(a, b, ((dims[0], dims[1]), ((), ())), preferred_element_type=F32)


def mix_heads(mix, values):
    return jnp.einsum("gh,hij->gij", mix, values, precision=lax.Precision.HIGH)


def norm_scale(values):
    return lax.rsqrt(jnp.mean(values * values, axis=-1, keepdims=True) + EPSILON)


def norm_back(values, gain, grad):
    scale = norm_scale(values)
    weighted = grad * gain
    inner = jnp.mean(values * weighted, axis=-1, keepdims=True)
    grad_values = scale * weighted - values * (scale * scale * scale) * inner
    grad_gain = jnp.sum(grad * values * scale, axis=0)
    return grad_values, grad_gain


def gelu_pair(values):
    inner = 0.7978845608028654 * (values + 0.044715 * values * values * values)
    tanh = jnp.tanh(inner)
    value = 0.5 * values * (1.0 + tanh)
    slope = 0.5 * (1.0 + tanh) + 0.5 * values * (1.0 - tanh * tanh) * (
        0.7978845608028654 * (1.0 + 3.0 * 0.044715 * values * values)
    )
    return value, slope


def forward(values, valid, params):
    w_query, w_key, w_value, w_output, w_in, w_out, gain_attn, gain_ffn, mix_pre, mix_post = params
    length, width = values.shape
    heads = mix_pre.shape[0]
    split = (length, heads, width // heads)
    normed = (values * norm_scale(values) * gain_attn).astype(BF16)
    query = dot(normed, w_query, ((1,), (0,))).astype(BF16).reshape(split)
    key = dot(normed, w_key, ((1,), (0,))).astype(BF16).reshape(split)
    value = dot(normed, w_value, ((1,), (0,))).astype(BF16).reshape(split)
    scores = jnp.einsum("ihd,jhd->hij", query, key, preferred_element_type=F32) * (split[2] ** -0.5)
    rows = lax.broadcasted_iota(jnp.int32, (length, length), 0)
    columns = lax.broadcasted_iota(jnp.int32, (length, length), 1)
    logits = jnp.where(columns <= rows, mix_heads(mix_pre, scores), MASKED)
    exponent = jnp.exp(logits - jnp.max(logits, axis=-1, keepdims=True))
    probs = exponent / jnp.sum(exponent, axis=-1, keepdims=True)
    weights = mix_heads(mix_post, probs).astype(BF16)
    head_out = jnp.einsum("hij,jhd->ihd", weights, value, preferred_element_type=F32)
    head_out = head_out.astype(BF16).reshape(length, width)
    branch_attn = dot(head_out, w_output, ((1,), (0,)))
    residual = values + branch_attn
    normed_ffn = (residual * norm_scale(residual) * gain_ffn).astype(BF16)
    pre_act = dot(normed_ffn, w_in, ((1,), (0,)))
    activation, slope = gelu_pair(pre_act)
    activation = activation.astype(BF16)
    branch_ffn = dot(activation, w_out, ((1,), (0,)))
    out = valid * (residual + branch_ffn)
    squares = jnp.stack(
        [
            jnp.sum(jnp.mean(out * out, axis=-1)),
            jnp.sum(valid[:, 0] * jnp.mean(branch_attn * branch_attn, axis=-1)),
            jnp.sum(valid[:, 0] * jnp.mean(branch_ffn * branch_ffn, axis=-1)),
        ]
    )
    saved = (
        normed, query, key, value, scores, probs, weights, head_out, residual, normed_ffn, activation, slope,
    )
    return out.astype(BF16), squares, saved


def backward_ffn(grad_sum, params, saved):
    w_in, w_out, gain_ffn = params[4], params[5], params[7]
    residual, normed_ffn, activation, slope = saved[8:]
    grad_branch = grad_sum.astype(BF16)
    grad_act = dot(grad_branch, w_out, ((1,), (1,)))
    grad_pre = (grad_act * slope).astype(BF16)
    grad_normed = dot(grad_pre, w_in, ((1,), (1,)))
    back, grad_gain = norm_back(residual, gain_ffn, grad_normed)
    return grad_sum + back, grad_gain, (activation, grad_branch, normed_ffn, grad_pre)


def backward_attention(values, grad_resid, params, saved):
    w_query, w_key, w_value, w_output = params[:4]
    gain_attn, mix_pre, mix_post = params[6], params[8], params[9]
    normed, query, key, value, scores, probs, weights, head_out = saved[:8]
    length, heads, size = query.shape
    grad_attn = grad_resid.astype(BF16)
    grad_heads = dot(grad_attn, w_output, ((1,), (1,))).astype(BF16).reshape(query.shape)
    grad_weights = jnp.einsum("ihd,jhd->hij", grad_heads, value, preferred_element_type=F32)
    grad_value = jnp.einsum("hij,ihd->jhd", weights, grad_heads, preferred_element_type=F32)
    grad_mix_post = jnp.einsum("gij,hij->gh", grad_weights, probs, precision=lax.Precision.HIGH)
    grad_probs = mix_heads(mix_post.T, grad_weights)
    grad_logits = probs * (grad_probs - jnp.sum(probs * grad_probs, axis=-1, keepdims=True))
    grad_mix_pre = jnp.einsum("gij,hij->gh", grad_logits, scores, precision=lax.Precision.HIGH)
    grad_scores = mix_heads(mix_pre.T, grad_logits).astype(BF16)
    scale = size**-0.5
    grad_query = jnp.einsum("hij,jhd->ihd", grad_scores, key, preferred_element_type=F32) * scale
    grad_key = jnp.einsum("hij,ihd->jhd", grad_scores, query, preferred_element_type=F32) * scale
    width = heads * size
    pieces = tuple(
        piece.astype(BF16).reshape(length, width) for piece in (grad_query, grad_key, grad_value)
    )
    grad_normed = sum(
        dot(piece, matrix, ((1,), (1,))) for piece, matrix in zip(pieces, (w_query, w_key, w_value))
    )
    back, grad_gain = norm_back(values, gain_attn, grad_normed)
    return grad_resid + back, grad_gain, grad_mix_pre, grad_mix_post, (normed, head_out, grad_attn) + pieces


def local(
    inputs, cotangent, lengths, w_query, w_key, w_value, w_output, w_in, w_out, gain_attn, gain_ffn, mix_pre, mix_post,
):
    core = lax.axis_index("section")
    is_first = core == 0
    swap = lambda shard: lax.ppermute(shard, "section", [(0, 1), (1, 0)])
    length, width = inputs.shape[2:]
    hidden = w_in.shape[2]

    own = (w_query, w_key, w_value, w_output, w_in, w_out, gain_attn, gain_ffn, mix_pre, mix_post)
    other = tuple(swap(weight) for weight in own)
    layers = (
        tuple(jnp.where(is_first, a, b)[0] for a, b in zip(own, other)),
        tuple(jnp.where(is_first, b, a)[0] for a, b in zip(own, other)),
    )
    take = lambda whole: lax.dynamic_index_in_dim(whole, core, 0, keepdims=False)[0]
    values = take(inputs).astype(F32)
    upstream = take(cotangent).astype(F32)
    valid = (lax.broadcasted_iota(jnp.int32, (length, 1), 0) < take(lengths)).astype(F32)

    outputs, squares, kept, starts = [], [], [], []
    layer_in = values
    for params in layers:
        starts.append(layer_in)
        rounded, square, saved = forward(layer_in, valid, params)
        outputs.append(rounded)
        squares.append(square)
        kept.append(saved)
        layer_in = rounded.astype(F32)

    def split_cols(array):
        half = array.shape[1] // 2
        mine = lax.dynamic_slice_in_dim(array, core * half, half, 1)
        theirs = lax.dynamic_slice_in_dim(array, (1 - core) * half, half, 1)
        return mine, theirs

    def both_rows(array):
        return jnp.concatenate([array, swap(array)], axis=0)

    def both_half(array):
        mine, theirs = split_cols(array)
        return jnp.concatenate([mine, swap(theirs)], axis=0)

    def weight_grad(left, right):
        return dot(left, right, ((0,), (0,))).astype(BF16)

    grads = [None, None]
    small = [None, None]
    input_grads = [None, None]
    for index in (1, 0):
        params, saved = layers[index], kept[index]
        grad_sum = valid * upstream
        grad_resid, gain_ffn_grad, ffn = backward_ffn(grad_sum, params, saved)
        activation, grad_branch, normed_ffn, grad_pre = ffn
        down = weight_grad(both_half(activation), both_rows(grad_branch))
        up = weight_grad(both_rows(normed_ffn), both_half(grad_pre))
        grad_in, gain_attn_grad, mix_pre_grad, mix_post_grad, attn = backward_attention(
            starts[index], grad_resid, params, saved
        )
        normed, head_out, grad_attn, grad_query, grad_key, grad_value = attn
        rows = both_rows(normed)
        sides = [weight_grad(rows, both_half(piece)) for piece in (grad_query, grad_key, grad_value)]
        sides.append(weight_grad(both_rows(head_out), both_half(grad_attn)))
        blocks = [down]
        blocks += [up[:, at * width : (at + 1) * width] for at in range(up.shape[1] // width)]
        blocks += [jnp.concatenate(sides[:2], axis=1), jnp.concatenate(sides[2:], axis=1)]
        grads[index] = jnp.concatenate(blocks, axis=0)
        small[index] = jnp.concatenate(
            [gain_attn_grad, gain_ffn_grad, mix_pre_grad.reshape(-1), mix_post_grad.reshape(-1), squares[index]]
        )
        input_grads[index] = grad_in.astype(BF16)
        upstream = input_grads[index].astype(F32)

    shards = [lax.psum_scatter(grad, "dp", scatter_dimension=0, tiled=True) for grad in grads]
    mine = jnp.where(is_first, shards[0], shards[1])
    theirs = swap(jnp.where(is_first, shards[1], shards[0]))
    halves = jnp.concatenate([jnp.where(is_first, mine, theirs), jnp.where(is_first, theirs, mine)], axis=0)
    whole = lax.all_gather(halves, "dp", axis=0)
    ranks = whole.shape[0]
    whole = whole.reshape(ranks, 2, -1, width).transpose(1, 0, 2, 3).reshape(2, -1, width).astype(F32)
    half = width // 2
    count = hidden // 2
    w_out_grad = whole[:, :count].reshape(1, hidden, width)
    blocks = (hidden // 2) // width
    up = whole[:, count : count + blocks * width].reshape(2 * blocks, width, width)
    w_in_grad = up.transpose(1, 0, 2).reshape(1, width, hidden)
    rest = whole[:, count + blocks * width :].reshape(2, 2, width, 2, half)
    rest = rest.transpose(1, 3, 2, 0, 4).reshape(4, 1, width, width)

    both = jnp.stack(small)
    total_small = jnp.where(is_first, both, both[::-1])
    mine_small = total_small[0] + swap(total_small[1])
    tail = jnp.concatenate([mine_small, jnp.sum(valid)[None] + swap(jnp.sum(valid)[None])])
    tail = lax.psum(tail, "dp")
    heads = mix_pre.shape[1]
    square = heads * heads
    at = 2 * width
    rms = jnp.sqrt(tail[at + 2 * square : at + 2 * square + 3] / tail[-1])[None]

    def place(pair):
        mine = jnp.where(is_first, pair[0], pair[1])
        theirs = swap(jnp.where(is_first, pair[1], pair[0]))
        ordered = [jnp.where(is_first, mine, theirs), jnp.where(is_first, theirs, mine)]
        return jnp.stack(ordered)[None, :, None]

    return (
        place(outputs),
        place(input_grads),
        rest[0],
        rest[1],
        rest[2],
        rest[3],
        w_in_grad,
        w_out_grad,
        tail[None, :width],
        tail[None, width:at],
        tail[at : at + square].reshape(1, heads, heads),
        tail[at + square : at + 2 * square].reshape(1, heads, heads),
        rms,
    )


def solution(mesh):
    in_specs = (
        P(None, "dp", None, None),
        P(None, "dp", None, None),
        P(None, "dp"),
        P("section", None, None),
        P("section", None, None),
        P("section", None, None),
        P("section", None, None),
        P("section", None, None),
        P("section", None, None),
        P("section", None),
        P("section", None),
        P("section", None, None),
        P("section", None, None),
    )
    out_specs = (
        P("section", None, "dp", None, None),
        P("section", None, "dp", None, None),
        P("section", None, None),
        P("section", None, None),
        P("section", None, None),
        P("section", None, None),
        P("section", None, None),
        P("section", None, None),
        P("section", None),
        P("section", None),
        P("section", None, None),
        P("section", None, None),
        P("section", None),
    )
    return jax.shard_map(local, mesh=mesh, in_specs=in_specs, out_specs=out_specs, check_vma=False)
```

time: 1710 us -> 801 us (0.47)
  waiting for transfers between devices: 1070 us -> 351 us
  matrix products: 360 us -> 167 us
  local copies, waits for them, and re-layouts: 108 us -> 160 us
  blocking collectives: 75.3 us -> 42 us
  other arithmetic: 60.6 us -> 41.5 us
    unnamed x8 -> x3, waiting for transfers between devices: 741 us -> 0.05 us
    reduce_scatter x0 -> x2, waiting for transfers between devices: none -> 288 us  [local(): lax.psum_scatter(grad, 'dp', scatter_dimension=0, tiled=True)]
    all_gather x6 -> x1, waiting for transfers between devices: 331 us -> 51.2 us  [local(): whole = lax.all_gather(halves, 'dp', axis=0)]
    dot_general x106 -> x60, matrix products: 360 us -> 167 us  [the longest x36 74.6 us: dot(): lax.dot_general(a, b, ((dims[0], dims[1]), ((), ())), preferred_element_t...]
    reshape x0 -> x9, local copies, waits for them, and re-layouts: none -> 43.6 us  [the longest x1 13.2 us: local(): rest = rest.transpose(1, 3, 2, 0, 4).reshape(4, 1, width, width)]
    another operation x6 -> x2, local copies, waits for them, and re-layouts: 35.6 us -> 0.02 us  [local(): both = jnp.stack(small)]
    psum x1, blocking collectives: 75.3 us -> 42 us  [local(): tail = lax.psum(tail, 'dp')]
    transpose x0 -> x2, local copies, waits for them, and re-layouts: none -> 30.6 us  [the longest x1 17.1 us: local(): rest = rest.transpose(1, 3, 2, 0, 4).reshape(4, 1, width, width)]
  transfers between devices with their start and end apart: 11 -> 38, of which waited for: 6 -> 9; matrix products, arithmetic and copies ran while one was open for 9% -> 30% of each run, Pallas kernels for 0% -> 0%
where the time goes in v1:
time: 801 us; the launch traced here: 790 us
  waiting for transfers between devices  351 us (44%)
  matrix products  167 us (21%)
  local copies, waits for them, and re-layouts  160 us (20%)
  blocking collectives  42 us (5%)
  other arithmetic  41.5 us (5%)
  between operations  17.6 us (2%)
  starting transfers between devices  10.7 us (1%)
    reduce_scatter x2, waiting for transfers between devices, local(): lax.psum_scatter(grad, 'dp', scatter_dimension=0, tiled=True)  288 us
    dot_general x36, matrix products, dot(): lax.dot_general(a, b, ((dims[0], dims[1]), ((), ())), preferred_element_t...  74.6 us
    all_gather x1, waiting for transfers between devices, local(): whole = lax.all_gather(halves, 'dp', axis=0)  51.2 us
    psum x1, blocking collectives, local(): tail = lax.psum(tail, 'dp')  42 us
    dot_general x8, matrix products, mix_heads(): return jnp.einsum('gh,hij->gij', mix, values, precision=lax.Precision.HIGH)  38.9 us
    slice x1, local copies, waits for them, and re-layouts, local(): w_out_grad = whole[:, :count].reshape(1, hidden, width)  20.8 us
    dot_general x2, matrix products, backward_attention(): jnp.einsum('gij,hij->gh', grad_logits, scores, precision=lax.Precision.HIGH)  19.6 us
    dot_general x2, matrix products, backward_attention(): jnp.einsum('gij,hij->gh', grad_weights, probs, precision=lax.Precision.HIGH)  17.8 us
  transfers between devices with their start and end apart: 38, of which 9 were waited for; matrix products, arithmetic and copies ran while one was open for 30% of the time, Pallas kernels for 0%

profile of v1, /device:TPU:0, one launch (start us, length us, event | category | flops | bytes accessed | tf_op | source)
XLA Modules:
  0.0 790.5 jit_solution(18255932944527995268)
XLA Ops:
  13.1 6.0 collective-permute-done.2
  28.9 3.0 convolution_convert_fusion.22
  38.2 4.2 select_reduce_fusion.1
  47.3 5.1 fusion.204
  58.0 6.3 multiply_convert_fusion.1
  76.9 4.2 select_reduce_fusion
  83.3 3.1 fusion.199
  90.1 4.2 multiply_convert_fusion
  94.5 5.9 fusion.38
  100.3 5.2 multiply_reduce_fusion.5
  105.5 5.8 fusion.246
  121.1 6.7 multiply_reduce_fusion.1
  127.9 4.3 fusion.74
  139.7 3.1 fusion.41
  156.8 7.0 multiply_reduce_fusion
  163.8 4.3 fusion.75
  210.6 132.9 %reduce-scatter.3.cloned.1.call-done = bf16[288,768]{1,0:T(8,128)(2,1)} async-done(((bf16[4608,768]{1,0:T(8,128)(2,1)}), bf16[288,768]{1,0:T(8,128)(2,1)}) %reduce-scatter.3.cloned.1.call-update) | async-done | bytes 442384 | tf_op jit(solution)/shard_map/reduce_scatter | solution.py:194
  343.5 155.1 %reduce-scatter.5.cloned.1.call-done = bf16[288,768]{1,0:T(8,128)(2,1)} async-done(((bf16[4608,768]{1,0:T(8,128)(2,1)}), bf16[288,768]{1,0:T(8,128)(2,1)}) %reduce-scatter.5.cloned.1.call-update) | async-done | bytes 442384 | tf_op jit(solution)/shard_map/reduce_scatter | solution.py:194
  510.7 9.0 %fusion.104 = f32[12,12]{1,0:T(8,128)} fusion(f32[12,256,256]{2,1,0:T(8,128)} %copy-done.30, f32[12,256,256]{2,0,1:T(8,128)} %copy-done.6, f32[12,256]{0,1:T(8,128)} %copy-done.83, f32[12,256]{0,1:T(8,128)} %copy-done.68, pred[256,256]{1,0:T(8,128)(4,1)} %iota_compare_fusion), kind=kOutput, calls=%fused_computation.176 | convolution fusion | flops 58982400 | bytes 6382144 | tf_op jit(solution)/shard_map/gij,hij->gh/dot_general | solution.py:102
  521.0 9.9 %fusion.113 = f32[12,12]{1,0:T(8,128)} fusion(f32[12,256,256]{2,1,0:T(8,128)S(1)} %convolution_multiply_fusion, f32[12,256,256]{2,0,1:T(8,128)} %copy-done.118, f32[12,256]{0,1:T(8,128)} %copy-done.120, f32[12,256,256]{2,0,1:T(8,128)} %copy-done.6, f32[12,256]{0,1:T(8,128)} %copy-done.83, f32[12,256]{0,1:T(8,128)} %copy-done.68, ...), kind=kOutput, calls=%fused_computation.179 | convolution fusion | flops 60555264 | bytes 9540160 | tf_op jit(solution)/shard_map/gij,hij->gh/dot_general | solution.py:105
  539.3 8.9 %fusion.107 = f32[12,12]{1,0:T(8,128)} fusion(f32[12,256,256]{2,1,0:T(8,128)} %copy-done.31, f32[12,256,256]{2,0,1:T(8,128)} %copy-done.4, f32[12,256]{0,1:T(8,128)} %copy-done.81, f32[12,256]{0,1:T(8,128)} %copy-done.66, pred[256,256]{1,0:T(8,128)(4,1)} %iota_compare_fusion), kind=kOutput, calls=%fused_computation.177 | convolution fusion | flops 58982400 | bytes 6382144 | tf_op jit(solution)/shard_map/gij,hij->gh/dot_general | solution.py:102
  549.6 9.7 %fusion.110 = f32[12,12]{1,0:T(8,128)} fusion(f32[12,256,256]{2,1,0:T(8,128)S(1)} %copy-done.3, f32[12,256,256]{2,0,1:T(8,128)} %copy-done.119, f32[12,256]{0,1:T(8,128)} %copy-done.121, f32[12,256,256]{2,0,1:T(8,128)} %copy-done.4, f32[12,256]{0,1:T(8,128)} %copy-done.81, f32[12,256]{0,1:T(8,128)} %copy-done.66, pred[256,256]{1,0:T(8,128)(4,1)} %iota_compare_fusion), kind=kOutput, calls=%fused_computation.178 | convolution fusion | flops 60555264 | bytes 9540160 | tf_op jit(solution)/shard_map/gij,hij->gh/dot_general | solution.py:105
  569.9 42.0 %psum.7 = f32[1828]{0:T(1024)S(1)} all-reduce(f32[1828]{0:T(1024)S(1)} %pad_maximum_fusion.10), channel_id=1, replica_groups=mesh['section'=2,'dp'=16] {'dp'}, use_global_device_ids=true, to_apply=%region_33.34 | all-reduce | flops 1828 | bytes 14624 | tf_op jit(solution)/shard_map/psum | solution.py:214
  619.5 51.2 %all-gather.3.cloned.1.call-done = bf16[9216,768]{1,0:T(8,128)(2,1)} async-done(((bf16[576,768]{1,0:T(8,128)(2,1)}), bf16[9216,768]{1,0:T(8,128)(2,1)}) %all-gather.3.cloned.1.call-update) | async-done | bytes 14155792 | tf_op jit(solution)/shard_map/all_gather | solution.py:198
  670.6 15.9 %copy.184 = f32[16,2,288,768]{3,2,0,1:T(8,128)} copy(bf16[16,2,288,768]{3,2,1,0:T(8,128)(2,1)} %bitcast.301) | data formatting | bytes 42467328 | tf_op jit(solution)/shard_map/convert_element_type | solution.py:200
  686.5 20.8 %fusion.250 = (f32[2,1536,768]{2,1,0:T(8,128)}, f32[2,1536,768]{2,1,0:T(8,128)}, f32[2,1536,768]{2,1,0:T(8,128)}) fusion(f32[2,4608,768]{2,1,0:T(8,128)} %bitcast.298), kind=kLoop, calls=%fused_computation.396 | loop fusion | bytes 56623104 | tf_op jit(solution)/shard_map/slice | solution.py:203
  707.3 13.4 %copy.186 = f32[768,4,768]{2,1,0:T(4,128)} copy(f32[768,4,768]{2,0,1:T(8,128)} %bitcast.299) | data formatting | bytes 18874368 | tf_op jit(solution)/shard_map/transpose | solution.py:206
  720.7 12.3 %reshape.281 = f32[1,768,3072]{2,1,0:T(8,128)} reshape(f32[768,4,768]{2,1,0:T(4,128)} %copy.186) | data formatting | bytes 18874368 | tf_op jit(solution)/shard_map/reshape | solution.py:206
  733.0 12.4 %reshape.278 = f32[2,2,768,2,384]{4,3,2,1,0:T(2,128)} reshape(f32[2,1536,768]{2,1,0:T(8,128)} %get-tuple-element.101) | data formatting | bytes 18874368 | tf_op jit(solution)/shard_map/reshape | solution.py:207
  745.4 17.1 %copy.185 = f32[2,2,768,2,384]{4,3,2,1,0:T(2,128)} copy(f32[2,2,768,2,384]{4,1,2,0,3:T(2,128)} %bitcast.300) | data formatting | bytes 18874368 | tf_op jit(solution)/shard_map/transpose | solution.py:208
  762.6 13.2 %reshape.279 = f32[4,1,768,768]{3,2,1,0:T(8,128)} reshape(f32[2,2,768,2,384]{4,3,2,1,0:T(2,128)} %copy.185) | data formatting | bytes 18874368 | tf_op jit(solution)/shard_map/reshape | solution.py:208
  775.8 7.6 slice_bitcast_fusion
  (477 shorter events, 163.1 us)
Async XLA Ops:
  7.2 336.3 %reduce-scatter.3.cloned.1.call-start = ((), (), s32[]{:S(2)}) async-start(), calls=%async_computation.2 | async-start | bytes 7520256 | tf_op jit(solution)/shard_map/reduce_scatter | solution.py:194
  7.3 21.5 %collective-permute-start.4 = (bf16[1,768,768]{2,1,0:T(8,128)(2,1)}, bf16[1,768,768]{2,1,0:T(8,128)(2,1)S(1)}, u32[]{:S(2)}, u32[]{:S(2)}) collective-permute-start(bf16[1,768,768]{2,1,0:T(8,128)(2,1)} %param.16), channel_id=1, source_target_pairs={{0,16},{16,0},{1,17},{17,1},{2,18},{18,2},{3,19},{19,3},{4,20},{20... | collective-permute-start | bytes 3538952 | tf_op jit(solution)/shard_map/ppermute | solution.py:126
  7.8 50.2 %collective-permute-start.8 = (bf16[1,768,3072]{2,1,0:T(8,128)(2,1)}, bf16[1,768,3072]{2,1,0:T(8,128)(2,1)}, u32[]{:S(2)}, u32[]{:S(2)}) collective-permute-start(bf16[1,768,3072]{2,1,0:T(8,128)(2,1)} %param.20), channel_id=1, source_target_pairs={{0,16},{16,0},{1,17},{17,1},{2,18},{18,2},{3,19},{19,3},{4,20},{20... | collective-permute-start | bytes 14155784 | tf_op jit(solution)/shard_map/ppermute | solution.py:126
  7.9 5.2 collective-permute-start.3
  8.3 10.8 %collective-permute-start.2 = (f32[1,12,12]{2,0,1:T(1,128)}, f32[1,12,12]{2,0,1:T(1,128)}, u32[]{:S(2)}, u32[]{:S(2)}) collective-permute-start(f32[1,12,12]{2,0,1:T(1,128)} %param.25), channel_id=1, source_target_pairs={{0,16},{16,0},{1,17},{17,1},{2,18},{18,2},{3,19},{19,3},{4,20},{20... | collective-permute-start | bytes 1736 | tf_op jit(solution)/shard_map/ppermute | solution.py:126
  8.4 23.5 %collective-permute-start.5 = (bf16[1,768,768]{2,1,0:T(8,128)(2,1)}, bf16[1,768,768]{2,1,0:T(8,128)(2,1)S(1)}, u32[]{:S(2)}, u32[]{:S(2)}) collective-permute-start(bf16[1,768,768]{2,1,0:T(8,128)(2,1)} %param.17), channel_id=1, source_target_pairs={{0,16},{16,0},{1,17},{17,1},{2,18},{18,2},{3,19},{19,3},{4,20},{20... | collective-permute-start | bytes 3538952 | tf_op jit(solution)/shard_map/ppermute | solution.py:126
  13.0 12.6 %collective-permute-start = (f32[1,768]{1,0:T(1,128)}, f32[1,768]{1,0:T(1,128)S(1)}, u32[]{:S(2)}, u32[]{:S(2)}) collective-permute-start(f32[1,768]{1,0:T(1,128)} %param.22), channel_id=1, source_target_pairs={{0,16},{16,0},{1,17},{17,1},{2,18},{18,2},{3,19},{19,3},{4,20},{20... | collective-permute-start | bytes 9224 | tf_op jit(solution)/shard_map/ppermute | solution.py:126
  19.0 8.0 %collective-permute-start.7 = (f32[1,768]{1,0:T(1,128)}, f32[1,768]{1,0:T(1,128)}, u32[]{:S(2)}, u32[]{:S(2)}) collective-permute-start(f32[1,768]{1,0:T(1,128)} %param.23), channel_id=1, source_target_pairs={{0,16},{16,0},{1,17},{17,1},{2,18},{18,2},{3,19},{19,3},{4,20},{20... | collective-permute-start | bytes 9224 | tf_op jit(solution)/shard_map/ppermute | solution.py:126
  26.1 20.3 %collective-permute-start.1 = (bf16[1,768,768]{2,1,0:T(8,128)(2,1)}, bf16[1,768,768]{2,1,0:T(8,128)(2,1)}, u32[]{:S(2)}, u32[]{:S(2)}) collective-permute-start(bf16[1,768,768]{2,1,0:T(8,128)(2,1)} %param.18), channel_id=1, source_target_pairs={{0,16},{16,0},{1,17},{17,1},{2,18},{18,2},{3,19},{19,3},{4,20},{20... | collective-permute-start | bytes 3538952 | tf_op jit(solution)/shard_map/ppermute | solution.py:126
  27.0 37.3 %collective-permute-start.9 = (bf16[1,3072,768]{2,1,0:T(8,128)(2,1)}, bf16[1,3072,768]{2,1,0:T(8,128)(2,1)}, u32[]{:S(2)}, u32[]{:S(2)}) collective-permute-start(bf16[1,3072,768]{2,1,0:T(8,128)(2,1)} %param.21), channel_id=1, source_target_pairs={{0,16},{16,0},{1,17},{17,1},{2,18},{18,2},{3,19},{19,3},{4,20},{20... | collective-permute-start | bytes 14155784 | tf_op jit(solution)/shard_map/ppermute | solution.py:126
  28.8 26.2 %collective-permute-start.6 = (bf16[1,768,768]{2,1,0:T(8,128)(2,1)}, bf16[1,768,768]{2,1,0:T(8,128)(2,1)}, u32[]{:S(2)}, u32[]{:S(2)}) collective-permute-start(bf16[1,768,768]{2,1,0:T(8,128)(2,1)} %param.19), channel_id=1, source_target_pairs={{0,16},{16,0},{1,17},{17,1},{2,18},{18,2},{3,19},{19,3},{4,20},{20... | collective-permute-start | bytes 3538952 | tf_op jit(solution)/shard_map/ppermute | solution.py:126
  53.9 121.6 %collective-permute-start.20 = (bf16[256,768]{0,1:T(8,128)(2,1)}, bf16[256,768]{0,1:T(8,128)(2,1)}, u32[]{:S(2)}, u32[]{:S(2)}) collective-permute-start(bf16[256,768]{0,1:T(8,128)(2,1)} %bitcast.10), channel_id=1, source_target_pairs={{0,16},{16,0},{1,17},{17,1},{2,18},{18,2},{3,19},{19,3},{4,20},{20... | collective-permute-start | bytes 1179656 | tf_op jit(solution)/shard_map/ppermute | solution.py:126
  169.5 11.9 %collective-permute-start.15 = (bf16[256,1536]{1,0:T(8,128)(2,1)S(1)}, bf16[256,1536]{1,0:T(8,128)(2,1)S(1)}, u32[]{:S(2)}, u32[]{:S(2)}) collective-permute-start(bf16[256,1536]{1,0:T(8,128)(2,1)S(1)} %copy-done.64), channel_id=1, source_target_pairs={{0,16},{16,0},{1,17},{17,1},{2,18},{18,2},{3,19},{19,3},{4,20},{20... | collective-permute-start | bytes 2359304 | tf_op jit(solution)/shard_map/ppermute | solution.py:126
  173.8 5.0 collective-permute-start.16
  175.6 7.3 collective-permute-start.12
  176.5 4.9 collective-permute-start.14
  176.9 2.9 collective-permute-start.19
  179.8 3.1 collective-permute-start.13
  190.2 308.5 %reduce-scatter.5.cloned.1.call-start = ((), (), s32[]{:S(2)}) async-start(), calls=%async_computation.3 | async-start | bytes 7520256 | tf_op jit(solution)/shard_map/reduce_scatter | solution.py:194
  190.4 7.7 collective-permute-start.26
  191.9 4.0 collective-permute-start.31
  193.3 2.9 collective-permute-start.29
  195.1 6.7 collective-permute-start.25
  195.5 2.3 collective-permute-start.28
  195.9 5.3 collective-permute-start.30
  196.3 7.0 collective-permute-start.22
  197.8 4.0 collective-permute-start.24
  200.3 2.9 collective-permute-start.23
  210.5 460.1 %all-gather.3.cloned.1.call-start = ((), (), s32[]{:S(2)}) async-start(), calls=%async_computation.4 | async-start | bytes 15040512 | tf_op jit(solution)/shard_map/all_gather | solution.py:198
  510.7 105.7 %collective-permute-start.10 = (bf16[256,768]{1,0:T(8,128)(2,1)}, bf16[256,768]{1,0:T(8,128)(2,1)}, u32[]{:S(2)}, u32[]{:S(2)}) collective-permute-start(bf16[256,768]{1,0:T(8,128)(2,1)} %broadcast_select_fusion.42), channel_id=1, source_target_pairs={{0,16},{16,0},{1,17},{17,1},{2,18},{18,2},{3,19},{19,3},{4,20},{20... | collective-permute-start | bytes 1179656 | tf_op jit(solution)/shard_map/ppermute | solution.py:126
  566.5 3.3 collective-permute-start.33
  569.7 48.7 %collective-permute-start.11 = (bf16[256,768]{1,0:T(8,128)(2,1)S(1)}, bf16[256,768]{1,0:T(8,128)(2,1)S(1)}, u32[]{:S(2)}, u32[]{:S(2)}) collective-permute-start(bf16[256,768]{1,0:T(8,128)(2,1)S(1)} %get-tuple-element.85), channel_id=1, source_target_pairs={{0,16},{16,0},{1,17},{17,1},{2,18},{18,2},{3,19},{19,3},{4,20},{20... | collective-permute-start | bytes 1179656 | tf_op jit(solution)/shard_map/ppermute | solution.py:126
  (138 other events, 978.0 us)
Sparse Core Ops, SparseCore 0:
  190.3 153.1 reduce-scatter.2
  349.4 149.1 reduce-scatter.4
  503.8 166.7 all-gather.2

commit v2 on v1

v2 whole, which is shorter than its diff:
```python
import functools

import jax
import jax.numpy as jnp
from jax import lax
from jax.experimental import pallas as pl
from jax.experimental.pallas import tpu as pltpu
from jax.sharding import PartitionSpec as P

EPSILON = 1e-06
MASKED = -1e30
F32 = jnp.float32
BF16 = jnp.bfloat16


HEADS_ROWS = 32
SPAN = 512


def row_scale(values):
    return lax.rsqrt(jnp.mean(values * values, axis=-1, keepdims=True) + EPSILON)


def norm_back(values, gain, grad):
    scale = row_scale(values)
    weighted = grad * gain
    inner = jnp.mean(values * weighted, axis=-1, keepdims=True)
    grad_values = scale * weighted - values * (scale * scale * scale) * inner
    return grad_values, jnp.sum(grad * values * scale, axis=0, keepdims=True)


def gelu_pair(values):
    square = values * values
    tanh = jnp.tanh(values * (0.7978845608028654 + 0.7978845608028654 * 0.044715 * square))
    half = 0.5 * (1.0 + tanh)
    slope = half + 0.5 * values * (1.0 - tanh * tanh) * (
        0.7978845608028654 + 3.0 * 0.7978845608028654 * 0.044715 * square
    )
    return values * half, slope


def dot_nn(left, right):
    return lax.dot_general(left, right, (((1,), (0,)), ((), ())), preferred_element_type=F32)


def dot_nt(left, right):
    return lax.dot_general(left, right, (((1,), (1,)), ((), ())), preferred_element_type=F32)


def dot_tn(left, right):
    return lax.dot_general(left, right, (((0,), (0,)), ((), ())), preferred_element_type=F32)


class Weight:
    def __init__(self, mine, own, other, held, sem):
        self.mine, self.own, self.other, self.held, self.sem = mine, own, other, held, sem

    def copy(self, source, cut):
        return pltpu.make_async_copy(source.at[(0,) + cut], self.held.at[cut], self.sem)

    def start(self, cut=(slice(None), slice(None))):
        @pl.when(self.mine)
        def _():
            self.copy(self.own, cut).start()

        @pl.when(jnp.logical_not(self.mine))
        def _():
            self.copy(self.other, cut).start()

    def wait(self, cut=(slice(None), slice(None))):
        self.copy(self.own, cut).wait()


def param_row(mine, own, other, at, count=1):
    rows = pl.ds(at, count)
    return jnp.where(mine, own[rows, :], other[rows, :])


def attention_kernel(
    layer, heads, meta, x, own_rows, other_rows, wq, wk, wv, wo, wq2, wk2, wv2, wo2,
    both_out, query_out, key_out, value_out, probs_out, residual_out, stats_out,
    held_q, held_k, held_v, held_o, total, sems,
):
    mine = meta[0] == layer
    weights = [
        Weight(mine, own, other, held, sems.at[at])
        for at, (own, other, held) in enumerate(
            ((wq, wq2, held_q), (wk, wk2, held_k), (wv, wv2, held_v), (wo, wo2, held_o))
        )
    ]
    for weight in weights:
        weight.start()
    length, width = x.shape
    half = length // 2
    values = x[...].astype(F32)
    gain = param_row(mine, own_rows, other_rows, 0)
    both_out[:, :width] = (values * row_scale(values) * gain).astype(BF16)
    for weight, held, out, factor in (
        (weights[0], held_q, query_out, (width // heads) ** -0.5),
        (weights[1], held_k, key_out, 1.0),
        (weights[2], held_v, value_out, 1.0),
    ):
        weight.wait()
        made = dot_nn(both_out[:, :width], held[...]).astype(BF16)
        out[...] = (made.astype(F32) * factor).astype(BF16) if factor != 1.0 else made
    total[...] = jnp.zeros_like(total)

    def softmax(logits, first):
        rows = lax.broadcasted_iota(jnp.int32, logits.shape, 0) + first
        columns = lax.broadcasted_iota(jnp.int32, logits.shape, 1)
        logits = jnp.where(columns <= rows, logits, MASKED)
        exponent = jnp.exp(logits - jnp.max(logits, axis=-1, keepdims=True))
        return exponent / jnp.sum(exponent, axis=-1, keepdims=True)

    def head(at, _):
        mixed = key_out[...].astype(F32) * param_row(mine, own_rows, other_rows, 2 + at)
        high = mixed.astype(BF16)
        low = (mixed - high.astype(F32)).astype(BF16)
        upper = dot_nt(query_out[:half, :], high[:half]) + dot_nt(query_out[:half, :], low[:half])
        lower = dot_nt(query_out[half:, :], high) + dot_nt(query_out[half:, :], low)
        row = pl.multiple_of(at * length, length)
        probs_out[pl.ds(row, half), :half] = softmax(upper, 0).astype(BF16)
        probs_out[pl.ds(row, half), half:] = jnp.zeros((half, length - half), BF16)
        probs_out[pl.ds(row + half, half), :] = softmax(lower, half).astype(BF16)
        scaled = (value_out[...].astype(F32) * param_row(mine, own_rows, other_rows, 2 + heads + at)).astype(BF16)
        total[:half, :] += dot_nn(probs_out[pl.ds(row, half), :half], scaled[:half])
        total[half:, :] += dot_nn(probs_out[pl.ds(row + half, half), :], scaled)
        return 0

    lax.fori_loop(0, heads, head, 0)
    both_out[:, width:] = total[...].astype(BF16)
    weights[3].wait()
    branch = dot_nn(both_out[:, width:], held_o[...])
    residual_out[...] = values + branch
    valid = lax.broadcasted_iota(jnp.int32, (length, 1), 0) < meta[1]
    stats_out[...] = jnp.broadcast_to(
        jnp.sum(jnp.where(valid, branch * branch, 0.0), axis=0, keepdims=True), stats_out.shape
    )


def ffn_kernel(
    layer, backward, meta, residual, own_rows, other_rows, w_in, w_out, w_in2, w_out2, *refs
):
    if backward:
        upstream, refs = refs[0], refs[1:]
        out, own_first, send_first, own_second, send_second, resid_out, stats_out = refs[:7]
        held_in, held_out, normed, act, total, pre_grad, branch_grad, back_total, sems, out_sems = refs[7:]
    else:
        out, own_first, send_first, slope_out, stats_out = refs[:5]
        held_in, held_out, normed, act, total, sems, out_sems = refs[5:]
    core = meta[0]
    mine = core == layer
    length, width = residual.shape
    hidden = held_in.shape[1]
    steps = hidden // SPAN
    half = hidden // 2
    cuts_in = [(slice(None), pl.ds(step * SPAN, SPAN)) for step in range(steps)]
    cuts_out = [(pl.ds(step * SPAN, SPAN), slice(None)) for step in range(steps)]
    ins = [Weight(mine, w_in, w_in2, held_in, sems.at[step]) for step in range(steps)]
    outs = [Weight(mine, w_out, w_out2, held_out, sems.at[steps + step]) for step in range(steps)]
    for step in range(steps):
        ins[step].start(cuts_in[step])
        outs[step].start(cuts_out[step])
    values = residual[...]
    normed[...] = (values * row_scale(values) * param_row(mine, own_rows, other_rows, 1)).astype(BF16)
    valid = lax.broadcasted_iota(jnp.int32, (length, 1), 0) < meta[1]
    copies = []

    def send(source, target, at):
        copy = pltpu.make_async_copy(source, target, out_sems.at[at])
        copy.start()
        copies.append(copy)

    send(normed, own_first.at[:, pl.ds(half, width)], 0)
    send(normed, send_first.at[:, pl.ds(half, width)], 1)
    if backward:
        branch_grad[...] = jnp.where(valid, upstream[...], jnp.zeros_like(upstream))
        send(branch_grad, own_second.at[:, pl.ds(half, width)], 2)
        send(branch_grad, send_second.at[:, pl.ds(half, width)], 3)
    for step in range(steps):
        span = pl.ds(step * SPAN, SPAN)
        ins[step].wait(cuts_in[step])
        made, slope = gelu_pair(dot_nn(normed[...], held_in[:, span]))
        act[:, span] = made.astype(BF16)
        outs[step].wait(cuts_out[step])
        part = dot_nn(act[:, span], held_out[span, :])
        total[...] = part if step == 0 else total[...] + part
        if backward:
            grad = (dot_nt(branch_grad[...], held_out[span, :]) * slope).astype(BF16)
            pre_grad[:, span] = grad
            part = dot_nt(pre_grad[:, span], held_in[:, span])
            back_total[...] = part if step == 0 else back_total[...] + part
        else:
            slope_out[:, span] = slope.astype(BF16)
    mine_at = pl.ds(pl.multiple_of(core * half, 128), half)
    other_at = pl.ds(pl.multiple_of((1 - core) * half, 128), half)
    send(act.at[:, mine_at], own_first.at[:, pl.ds(0, half)], 4)
    send(act.at[:, other_at], send_first.at[:, pl.ds(0, half)], 5)
    if backward:
        send(pre_grad.at[:, mine_at], own_second.at[:, pl.ds(0, half)], 6)
        send(pre_grad.at[:, other_at], send_second.at[:, pl.ds(0, half)], 7)
    branch = total[...]
    made = jnp.where(valid, residual[...] + branch, 0.0)
    out[...] = made.astype(BF16)
    stats_out[0:1, :] = jnp.sum(made * made, axis=0, keepdims=True)
    stats_out[1:2, :] = jnp.sum(jnp.where(valid, branch * branch, 0.0), axis=0, keepdims=True)
    if backward:
        back, gain_grad = norm_back(
            residual[...], param_row(mine, own_rows, other_rows, 1), back_total[...]
        )
        resid_out[...] = branch_grad[...].astype(F32) + back
        stats_out[2:3, :] = gain_grad
    for copy in copies:
        copy.wait()


def ffn_back_kernel(
    layer, meta, residual, upstream, slope, own_rows, other_rows, w_in, w_out, w_in2, w_out2,
    own_second, send_second, resid_out, stats_out,
    held_in, held_out, pre_grad, branch_grad, back_total, sems, out_sems,
):
    core = meta[0]
    mine = core == layer
    length, width = residual.shape
    hidden = held_in.shape[1]
    steps = hidden // SPAN
    half = hidden // 2
    cuts_in = [(slice(None), pl.ds(step * SPAN, SPAN)) for step in range(steps)]
    cuts_out = [(pl.ds(step * SPAN, SPAN), slice(None)) for step in range(steps)]
    ins = [Weight(mine, w_in, w_in2, held_in, sems.at[step]) for step in range(steps)]
    outs = [Weight(mine, w_out, w_out2, held_out, sems.at[steps + step]) for step in range(steps)]
    for step in range(steps):
        outs[step].start(cuts_out[step])
        ins[step].start(cuts_in[step])
    valid = lax.broadcasted_iota(jnp.int32, (length, 1), 0) < meta[1]
    branch_grad[...] = jnp.where(valid, upstream[...], jnp.zeros_like(upstream))
    copies = []

    def send(source, target, at):
        copy = pltpu.make_async_copy(source, target, out_sems.at[at])
        copy.start()
        copies.append(copy)

    send(branch_grad, own_second.at[:, pl.ds(half, width)], 0)
    send(branch_grad, send_second.at[:, pl.ds(half, width)], 1)
    for step in range(steps):
        span = pl.ds(step * SPAN, SPAN)
        outs[step].wait(cuts_out[step])
        grad = dot_nt(branch_grad[...], held_out[span, :]) * slope[:, span].astype(F32)
        pre_grad[:, span] = grad.astype(BF16)
        ins[step].wait(cuts_in[step])
        part = dot_nt(pre_grad[:, span], held_in[:, span])
        back_total[...] = part if step == 0 else back_total[...] + part
    send(pre_grad.at[:, pl.ds(pl.multiple_of(core * half, 128), half)], own_second.at[:, pl.ds(0, half)], 2)
    send(pre_grad.at[:, pl.ds(pl.multiple_of((1 - core) * half, 128), half)], send_second.at[:, pl.ds(0, half)], 3)
    back, gain_grad = norm_back(residual[...], param_row(mine, own_rows, other_rows, 1), back_total[...])
    resid_out[...] = branch_grad[...].astype(F32) + back
    stats_out[0:1, :] = gain_grad
    for copy in copies:
        copy.wait()


def attention_back_kernel(
    layer, heads, meta, x, resid_grad, query, key, value, probs, own_rows, other_rows,
    wq, wk, wv, wo, wq2, wk2, wv2, wo2,
    own_pack, send_pack, grad_out, stats_out,
    held_q, held_k, held_v, held_o, attn_grad, head_grad, logit_grad, heads_scaled, query_scaled,
    query_grad, piece, total, sems, out_sems,
):
    core = meta[0]
    mine = core == layer
    weights = [
        Weight(mine, own, other, held, sems.at[at])
        for at, (own, other, held) in enumerate(
            ((wo, wo2, held_o), (wq, wq2, held_q), (wk, wk2, held_k), (wv, wv2, held_v))
        )
    ]
    for weight in weights:
        weight.start()
    length, width = x.shape
    half = width // 2
    copies = []

    def send(source, at, sem):
        for target, which in ((own_pack, core), (send_pack, 1 - core)):
            copy = pltpu.make_async_copy(
                source.at[:, pl.ds(pl.multiple_of(which * half, 128), half)],
                target.at[:, pl.ds(at * half, half)],
                out_sems.at[sem + (0 if target is own_pack else 1)],
            )
            copy.start()
            copies.append(copy)

    attn_grad[...] = resid_grad[...].astype(BF16)
    send(attn_grad, 3, 0)
    weights[0].wait()
    head_grad[...] = dot_nt(attn_grad[...], held_o[...]).astype(BF16)
    query_grad[...] = jnp.zeros_like(query_grad)

    def head(at, _):
        row = pl.multiple_of(at * length, length)
        rows = pl.ds(row, length)
        pre = param_row(mine, own_rows, other_rows, 2 + at)
        post = param_row(mine, own_rows, other_rows, 2 + heads + at)
        scaled = (value[...].astype(F32) * post).astype(BF16)
        grad_probs = dot_nt(head_grad[...], scaled)
        prob = probs[rows, :].astype(F32)
        inner = jnp.sum(prob * grad_probs, axis=-1, keepdims=True)
        logit_grad[rows, :] = (prob * (grad_probs - inner)).astype(BF16)
        heads_scaled[rows, :] = (head_grad[...].astype(F32) * post).astype(BF16)
        query_scaled[rows, :] = (query[...].astype(F32) * pre).astype(BF16)
        weighed = dot_nn(probs[rows, :], value[...])
        stats_out[pl.ds(HEADS_ROWS // 2 + at, 1), :] = jnp.sum(
            weighed * head_grad[...].astype(F32), axis=0, keepdims=True
        )
        routed = dot_nn(logit_grad[rows, :], key[...])
        stats_out[pl.ds(at, 1), :] = jnp.sum(routed * query[...].astype(F32), axis=0, keepdims=True)
        query_grad[...] += routed * pre
        return 0

    lax.fori_loop(0, heads, head, 0)
    factor = (width // heads) ** -0.5
    piece[0] = (query_grad[...] * factor).astype(BF16)
    send(piece.at[0], 0, 2)
    weights[1].wait()
    total[...] = dot_nt(piece[0], held_q[...])
    piece[1] = dot_tn(logit_grad[...], query_scaled[...]).astype(BF16)
    send(piece.at[1], 1, 4)
    weights[2].wait()
    total[...] += dot_nt(piece[1], held_k[...])
    piece[2] = dot_tn(probs[...], heads_scaled[...]).astype(BF16)
    send(piece.at[2], 2, 6)
    weights[3].wait()
    back, gain_grad = norm_back(
        x[...].astype(F32),
        param_row(mine, own_rows, other_rows, 0),
        total[...] + dot_nt(piece[2], held_v[...]),
    )
    grad_out[...] = (resid_grad[...] + back).astype(BF16)
    stats_out[pl.ds(heads, 1), :] = gain_grad
    for copy in copies:
        copy.wait()


def vmem():
    return pl.BlockSpec(memory_space=pltpu.VMEM)


def smem():
    return pl.BlockSpec(memory_space=pltpu.SMEM)


def shaped(shape, kind):
    return jax.ShapeDtypeStruct(shape, kind)


def call(kernel, in_specs, outs, out_specs, scratch, flops, bytes_accessed):
    return pl.pallas_call(
        kernel,
        out_shape=outs,
        in_specs=in_specs,
        out_specs=out_specs,
        scratch_shapes=scratch,
        compiler_params=pltpu.CompilerParams(vmem_limit_bytes=56 << 20),
        cost_estimate=pl.CostEstimate(flops=flops, bytes_accessed=bytes_accessed, transcendentals=0),
    )


def attention_forward(layer, heads, meta, x, rows, weights):
    length, width = x.shape
    square = length * width
    outs = (
        shaped((length, 2 * width), BF16),
        shaped((length, width), BF16),
        shaped((length, width), BF16),
        shaped((length, width), BF16),
        shaped((heads * length, length), BF16),
        shaped((length, width), F32),
        shaped((8, width), F32),
    )
    scratch = [pltpu.VMEM((width, width), BF16)] * 4
    scratch += [pltpu.VMEM((length, width), F32), pltpu.SemaphoreType.DMA((4,))]
    kernel = functools.partial(attention_kernel, layer, heads)
    run = call(
        kernel, [smem(), vmem(), vmem(), vmem()] + [hbm()] * 8, outs, [vmem()] * 7, scratch,
        8 * square * width + 6 * heads * length * square, 8 * width * width + 20 * square,
    )
    own, other = weights
    return run(meta, x, *rows, *own[:4], *other[:4])


def ffn_forward(layer, meta, residual, rows, weights, upstream=None):
    length, width = residual.shape
    hidden = weights[0][4].shape[2]
    half = hidden // 2
    pack = shaped((length, half + width), BF16)
    steps = hidden // SPAN
    held = [pltpu.VMEM((width, hidden), BF16), pltpu.VMEM((hidden, width), BF16)]
    held += [pltpu.VMEM((length, width), BF16), pltpu.VMEM((length, hidden), BF16), pltpu.VMEM((length, width), F32)]
    sems = [pltpu.SemaphoreType.DMA((2 * steps,)), pltpu.SemaphoreType.DMA((8,))]
    ins = [smem(), vmem(), vmem(), vmem()] + [hbm()] * 4
    work = 4 * length * width * hidden
    moved = 4 * width * hidden + 8 * length * hidden
    own, other = weights
    args = (meta, residual) + rows + own[4:6] + other[4:6]
    if upstream is None:
        outs = (shaped((length, width), BF16), pack, pack, shaped((length, hidden), BF16), shaped((8, width), F32))
        specs = [vmem(), hbm(), hbm(), vmem(), vmem()]
        return call(functools.partial(ffn_kernel, layer, False), ins, outs, specs, held + sems, work, moved)(*args)
    outs = (shaped((length, width), BF16), pack, pack, pack, pack, shaped((length, width), F32), shaped((8, width), F32))
    specs = [vmem()] + [hbm()] * 4 + [vmem()] * 2
    held += [pltpu.VMEM((length, hidden), BF16), pltpu.VMEM((length, width), BF16), pltpu.VMEM((length, width), F32)]
    kernel = functools.partial(ffn_kernel, layer, True)
    return call(kernel, ins + [vmem()], outs, specs, held + sems, 2 * work, moved)(*args, upstream)


def ffn_backward(layer, meta, residual, upstream, slope, rows, weights):
    length, width = residual.shape
    hidden = slope.shape[1]
    pack = shaped((length, hidden // 2 + width), BF16)
    steps = hidden // SPAN
    scratch = [pltpu.VMEM((width, hidden), BF16), pltpu.VMEM((hidden, width), BF16)]
    scratch += [pltpu.VMEM((length, hidden), BF16), pltpu.VMEM((length, width), BF16), pltpu.VMEM((length, width), F32)]
    scratch += [pltpu.SemaphoreType.DMA((2 * steps,)), pltpu.SemaphoreType.DMA((4,))]
    own, other = weights
    return call(
        functools.partial(ffn_back_kernel, layer),
        [smem()] + [vmem()] * 5 + [hbm()] * 4,
        (pack, pack, shaped((length, width), F32), shaped((8, width), F32)),
        [hbm(), hbm(), vmem(), vmem()],
        scratch,
        4 * length * width * hidden,
        4 * width * hidden + 6 * length * hidden,
    )(meta, residual, upstream, slope, *rows, *own[4:6], *other[4:6])


def attention_backward(layer, heads, meta, x, resid_grad, saved, rows, weights):
    length, width = x.shape
    square = length * width
    pack = shaped((length, 2 * width), BF16)
    scratch = [pltpu.VMEM((width, width), BF16)] * 4
    scratch += [pltpu.VMEM((length, width), BF16)] * 2
    scratch += [pltpu.VMEM((heads * length, length), BF16)]
    scratch += [pltpu.VMEM((heads * length, width), BF16)] * 2
    scratch += [pltpu.VMEM((length, width), F32), pltpu.VMEM((3, length, width), BF16), pltpu.VMEM((length, width), F32)]
    scratch += [pltpu.SemaphoreType.DMA((4,)), pltpu.SemaphoreType.DMA((8,))]
    own, other = weights
    return call(
        functools.partial(attention_back_kernel, layer, heads),
        [smem()] + [vmem()] * 8 + [hbm()] * 8,
        (pack, pack, shaped((length, width), BF16), shaped((HEADS_ROWS, width), F32)),
        [hbm(), hbm(), vmem(), vmem()],
        scratch,
        8 * square * width + 10 * heads * length * square,
        8 * width * width + 24 * square,
    )(meta, x, resid_grad, *saved, *rows, *own[:4], *other[:4])


BLOCKS = 8
HALF_BLOCKS = BLOCKS // 2
FFN_BITS = ((1, 2), (2, 4), (4, 1))
ATTN_BITS = ((4, 4), (1, 1), (2, 2))


def hbm():
    return pl.BlockSpec(memory_space=pl.ANY)


def block_shift(bits, core, rank):
    shift = 0
    for pair in bits:
        on = jnp.where(core == 0, (rank & pair[0]) != 0, (rank & pair[1]) != 0)
        shift = shift * 2 + on.astype(jnp.int32)
    return shift


def exchange(array, bits):
    count = lax.axis_size("dp")
    pairs = [(at, at ^ bits[0]) for at in range(count)]
    pairs += [(count + at, count + (at ^ bits[1])) for at in range(count)]
    return lax.ppermute(array, ("section", "dp"), pairs)


def add(left, right):
    return (left.astype(F32) + right.astype(F32)).astype(BF16)


def two_dots(own, other, right_own, right_other):
    return (dot_tn(own, right_own) + dot_tn(other, right_other)).astype(BF16)


def ffn_grad_kernel(shift_ref, first, first2, second, second2, send, keep):
    step = pl.program_id(0)
    relative = (step + HALF_BLOCKS) % BLOCKS
    block = relative ^ shift_ref[0]
    rows, width = keep.shape
    half = first.shape[1] - width

    def emit(value):
        @pl.when(step < HALF_BLOCKS)
        def _():
            send[...] = value

        @pl.when(step >= HALF_BLOCKS)
        def _():
            keep[...] = value

    per = width // rows
    place = jnp.maximum(block - HALF_BLOCKS, 0)
    down = block < HALF_BLOCKS
    left = pl.ds(pl.multiple_of(jnp.where(down, block * rows, half + (place % per) * rows), 128), rows)
    right = pl.ds(pl.multiple_of(jnp.where(down, half, (place // per) * width), 128), width)
    emit(two_dots(first[:, left], first2[:, left], second[:, right], second2[:, right]))


def attn_grad_kernel(shift_ref, both, both2, pack, pack2, send, keep):
    step = pl.program_id(0)
    relative = (step + HALF_BLOCKS) % BLOCKS
    block = relative ^ shift_ref[0]
    rows = keep.shape[0]
    which = block // 2
    left = pl.ds(pl.multiple_of(jnp.where(which == 3, 2 * rows, 0) + (block % 2) * rows, 128), rows)
    right = pl.ds(pl.multiple_of(which * rows, 128), rows)
    value = two_dots(both[:, left], both2[:, left], pack[:, right], pack2[:, right])

    @pl.when(step < HALF_BLOCKS)
    def _():
        send[...] = value

    @pl.when(step >= HALF_BLOCKS)
    def _():
        keep[...] = value


def grad_blocks(kernel, shift, factors, rows, width):
    whole = lambda array: pl.BlockSpec(array.shape, lambda step, shift_ref: (0, 0))
    out = jax.ShapeDtypeStruct((HALF_BLOCKS * rows, width), BF16)
    tokens = 2 * factors[0].shape[0]
    return pl.pallas_call(
        kernel,
        out_shape=(out, out),
        grid_spec=pltpu.PrefetchScalarGridSpec(
            num_scalar_prefetch=1,
            grid=(BLOCKS,),
            in_specs=[whole(array) for array in factors],
            out_specs=[
                pl.BlockSpec((rows, width), lambda step, shift_ref: (jnp.minimum(step, HALF_BLOCKS - 1), 0)),
                pl.BlockSpec((rows, width), lambda step, shift_ref: (jnp.maximum(step - HALF_BLOCKS, 0), 0)),
            ],
        ),
        compiler_params=pltpu.CompilerParams(vmem_limit_bytes=48 << 20),
        cost_estimate=pl.CostEstimate(
            flops=2 * tokens * BLOCKS * rows * width, bytes_accessed=2 * BLOCKS * rows * width, transcendentals=0
        ),
    )(shift.reshape(1), *factors)


def reduce_blocks(send, keep, bits):
    for at, pair in enumerate(bits):
        got = exchange(send, pair)
        if at + 1 < len(bits):
            half = keep.shape[0] // 2
            send, keep = add(keep[half:], got[half:]), add(keep[:half], got[:half])
        else:
            total = add(keep, got)
    return total


def finish_sum(total):
    bit = 8
    while bit < lax.axis_size("dp"):
        total = add(total, exchange(total, (bit, bit)))
        bit *= 2
    return total


def gather_blocks(total, bits):
    for pair in bits[:0:-1]:
        total = jnp.concatenate([total, exchange(total, pair)], axis=0)
    return total, exchange(total, bits[0])


def unpack_kernel(place, meta, *refs):
    sources, rest = refs[:8], refs[8:]
    outs, (taken, given, taken_sem, given_sem) = rest[:-4], rest[-4:]
    core = meta[0]
    rows = taken.shape[1]
    steps = 2 * BLOCKS

    def fetch(step):
        half, relative = divmod(step, BLOCKS)
        slot = step % 2
        for layer in range(2):
            for swapped in range(2):
                source = sources[4 * layer + 2 * swapped + relative // HALF_BLOCKS]
                window = source.at[pl.ds((relative % HALF_BLOCKS) * rows, rows)]

                @pl.when((core == layer) & ((half == core) == (swapped == 0)))
                def _():
                    pltpu.make_async_copy(window, taken.at[slot], taken_sem.at[slot]).start()

    def store(step, start):
        half, relative = divmod(step, BLOCKS)
        slot = step % 2
        block = relative ^ meta[1 + half]
        for chosen, window in place(half, block, outs):
            @pl.when(chosen)
            def _():
                copy = pltpu.make_async_copy(given.at[slot], window, given_sem.at[slot])
                copy.start() if start else copy.wait()

    fetch(0)
    for step in range(steps):
        slot = step % 2
        if step + 1 < steps:
            fetch(step + 1)
        pltpu.make_async_copy(sources[0].at[pl.ds(0, rows)], taken.at[slot], taken_sem.at[slot]).wait()
        if step >= 2:
            store(step - 2, False)
        given[slot] = taken[slot].astype(F32)
        store(step, True)
    store(steps - 2, False)
    store(steps - 1, False)


def place_ffn(half, block, outs):
    grad_in, grad_out = outs
    width, hidden = grad_in.shape[1:]
    rows = hidden // BLOCKS
    per = width // rows
    inner = jnp.maximum(block - HALF_BLOCKS, 0)
    at_out = pl.multiple_of(half * (hidden // 2) + jnp.minimum(block, HALF_BLOCKS - 1) * rows, rows)
    at_row = pl.multiple_of((inner % per) * rows, rows)
    at_column = pl.multiple_of(half * (hidden // 2) + (inner // per) * width, 128)
    return [
        (block < HALF_BLOCKS, grad_out.at[0, pl.ds(at_out, rows), :]),
        (block >= HALF_BLOCKS, grad_in.at[0, pl.ds(at_row, rows), pl.ds(at_column, width)]),
    ]


def place_attn(half, block, outs):
    width = outs[0].shape[1]
    rows = width // 2
    at_row = pl.multiple_of((block % 2) * rows, rows)
    return [
        (block // 2 == which, outs[which].at[0, pl.ds(at_row, rows), pl.ds(half * rows, rows)]) for which in range(4)
    ]


def unpack(place, meta, sources, outs):
    rows = sources[0].shape[0] // HALF_BLOCKS
    width = sources[0].shape[1]
    return pl.pallas_call(
        functools.partial(unpack_kernel, place),
        out_shape=outs,
        in_specs=[pl.BlockSpec(memory_space=pltpu.SMEM)] + [hbm()] * 8,
        out_specs=[hbm()] * len(outs),
        scratch_shapes=[
            pltpu.VMEM((2, rows, width), BF16),
            pltpu.VMEM((2, rows, width), F32),
            pltpu.SemaphoreType.DMA((2,)),
            pltpu.SemaphoreType.DMA((2,)),
        ],
        compiler_params=pltpu.CompilerParams(vmem_limit_bytes=32 << 20),
        cost_estimate=pl.CostEstimate(
            flops=0, bytes_accessed=12 * BLOCKS * rows * width, transcendentals=0
        ),
    )(meta, *sources)


def after(values, done):
    return lax.optimization_barrier(tuple(values) + tuple(done))[: len(values)]


def param_rows(gain_attn, gain_ffn, mix_pre, mix_post):
    heads = mix_pre.shape[1]
    width = gain_attn.shape[1]
    spread = lambda mix: jnp.repeat(mix, width // heads, axis=1)
    rows = jnp.concatenate([gain_attn, gain_ffn, spread(mix_pre[0]), spread(mix_post[0].T)], axis=0)
    return jnp.pad(rows, ((0, HEADS_ROWS - rows.shape[0]), (0, 0)))


def local(
    inputs, cotangent, lengths, w_query, w_key, w_value, w_output, w_in, w_out, gain_attn, gain_ffn, mix_pre, mix_post,
):
    core = lax.axis_index("section")
    rank = lax.axis_index("dp")
    is_first = core == 0
    swap = lambda shard: lax.ppermute(shard, "section", [(0, 1), (1, 0)])
    length, width = inputs.shape[2:]
    hidden = w_in.shape[2]
    heads = mix_pre.shape[1]

    own_rows = param_rows(gain_attn, gain_ffn, mix_pre, mix_post)
    own = (w_query, w_key, w_value, w_output, w_in, w_out)
    other_rows = swap(own_rows)
    other = tuple(swap(weight) for weight in own[:4])
    other += tuple(swap(weight) for weight in after(own[4:], other))
    rows = (own_rows, other_rows)
    weights = (own, other)
    take = lambda whole: lax.dynamic_index_in_dim(whole, core, 0, keepdims=False)[0]
    count = take(lengths)
    meta = jnp.stack([core, count]).astype(jnp.int32)

    ffn_shift = block_shift(FFN_BITS, core, rank)
    attn_shift = block_shift(ATTN_BITS, core, rank)

    def ffn_blocks(first, second):
        factors = (first[0], swap(first[1]), second[0], swap(second[1]))
        return grad_blocks(ffn_grad_kernel, ffn_shift, factors, hidden // BLOCKS, width)

    def attn_blocks(both, pack):
        factors = (both, swap(both), pack[0], swap(pack[1]))
        return grad_blocks(attn_grad_kernel, attn_shift, factors, width // 2, width // 2)

    start0 = take(inputs)
    both0, *qkvp0, residual0, stats_a0 = attention_forward(0, heads, meta, start0, rows, weights)
    mid, own0, send0, slope0, stats_f0 = ffn_forward(0, meta, residual0, rows, weights)
    both1, *qkvp1, residual1, stats_a1 = attention_forward(1, heads, meta, mid, rows, weights)
    last, own1, send1, own1b, send1b, resid1, stats_f1 = ffn_forward(
        1, meta, residual1, rows, weights, take(cotangent)
    )
    ffn1 = ffn_blocks((own1, send1), (own1b, send1b))
    (resid1,) = after((resid1,), ffn1)
    pack1, send_pack1, grad1, stats_b1 = attention_backward(1, heads, meta, mid, resid1, qkvp1, rows, weights)
    own0b, send0b, resid0, stats_g0 = ffn_backward(0, meta, residual0, grad1, slope0, rows, weights)
    (both1,) = after((both1,), (resid0,))
    attn1 = attn_blocks(both1, (pack1, send_pack1))
    (own0,) = after((own0,), attn1)
    ffn0 = ffn_blocks((own0, send0), (own0b, send0b))
    (resid0,) = after((resid0,), ffn0)
    pack0, send_pack0, grad0, stats_b0 = attention_backward(0, heads, meta, start0, resid0, qkvp0, rows, weights)
    attn0 = attn_blocks(both0, (pack0, send_pack0))

    gathered = [None, None]
    for index, ffn_pair, attn_pair in ((1, ffn1, attn1), (0, ffn0, attn0)):
        ffn_sum = finish_sum(reduce_blocks(*ffn_pair, FFN_BITS))
        attn_sum = finish_sum(reduce_blocks(*attn_pair, ATTN_BITS))
        ffn_parts = gather_blocks(ffn_sum, FFN_BITS)
        attn_parts = gather_blocks(attn_sum, ATTN_BITS)
        hand = lambda array: lax.ppermute(array, "section", [(1 - index, index)])
        gathered[index] = (
            ffn_parts + tuple(hand(part) for part in ffn_parts),
            attn_parts + tuple(hand(part) for part in attn_parts),
        )

    def shifts(bits):
        return jnp.stack([core, block_shift(bits, 0, rank), block_shift(bits, 1, rank)]).astype(jnp.int32)

    w_in_grad, w_out_grad = unpack(
        place_ffn,
        shifts(FFN_BITS),
        gathered[0][0] + gathered[1][0],
        (jax.ShapeDtypeStruct(w_in.shape, F32), jax.ShapeDtypeStruct(w_out.shape, F32)),
    )
    rest = unpack(
        place_attn,
        shifts(ATTN_BITS),
        gathered[0][1] + gathered[1][1],
        tuple(jax.ShapeDtypeStruct(w_query.shape, F32) for _ in range(4)),
    )

    def small_sums(back, gain_row, attn_row, ffn_rows):
        mixes = back.reshape(HEADS_ROWS, heads, width // heads).sum(axis=-1)
        at = HEADS_ROWS // 2
        squares = jnp.stack([ffn_rows[0], attn_row, ffn_rows[1]]).sum(axis=-1) / width
        return [back[heads], gain_row, mixes[:heads].reshape(-1), mixes[at : at + heads].T.reshape(-1), squares]

    parts = small_sums(stats_b0, stats_g0[0], stats_a0[0], stats_f0)
    parts += small_sums(stats_b1, stats_f1[2], stats_a1[0], stats_f1)
    tail = jnp.concatenate(parts + [count[None].astype(F32)])
    size = tail.shape[0]
    tail = jnp.pad(tail, (0, -size % 1024)).reshape(-1, 128)
    tail = tail + swap(tail)
    bit = 1
    while bit < lax.axis_size("dp"):
        tail = tail + exchange(tail, (bit, bit))
        bit *= 2
    tail = tail.reshape(-1)
    tokens = tail[size - 1]
    each = (size - 1) // 2
    tail = jnp.where(is_first, tail[:each], tail[each : 2 * each])
    square = heads * heads
    at = 2 * width
    rms = jnp.sqrt(tail[at + 2 * square : at + 2 * square + 3] / tokens)[None]

    def put(pair):
        mine = jnp.where(is_first, pair[0], pair[1])
        theirs = swap(jnp.where(is_first, pair[1], pair[0]))
        ordered = [jnp.where(is_first, mine, theirs), jnp.where(is_first, theirs, mine)]
        return jnp.stack(ordered)[None, :, None]

    return (
        put((mid, last)),
        put((grad0, grad1)),
        rest[0],
        rest[1],
        rest[2],
        rest[3],
        w_in_grad,
        w_out_grad,
        tail[None, :width],
        tail[None, width:at],
        tail[at : at + square].reshape(1, heads, heads),
        tail[at + square : at + 2 * square].reshape(1, heads, heads),
        rms,
    )


def solution(mesh):
    in_specs = (
        P(None, "dp", None, None),
        P(None, "dp", None, None),
        P(None, "dp"),
        P("section", None, None),
        P("section", None, None),
        P("section", None, None),
        P("section", None, None),
        P("section", None, None),
        P("section", None, None),
        P("section", None),
        P("section", None),
        P("section", None, None),
        P("section", None, None),
    )
    out_specs = (
        P("section", None, "dp", None, None),
        P("section", None, "dp", None, None),
        P("section", None, None),
        P("section", None, None),
        P("section", None, None),
        P("section", None, None),
        P("section", None, None),
        P("section", None, None),
        P("section", None),
        P("section", None),
        P("section", None, None),
        P("section", None, None),
        P("section", None),
    )
    return jax.shard_map(local, mesh=mesh, in_specs=in_specs, out_specs=out_specs, check_vma=False)
```

time: 801 us -> 486 us (0.61)
  matrix products: 167 us -> 0 us
  Pallas kernels: 0 us -> 163 us
  waiting for transfers between devices: 351 us -> 199 us
  local copies, waits for them, and re-layouts: 160 us -> 29.4 us
  starting transfers between devices: 10.7 us -> 56.1 us
  blocking collectives: 42 us -> 0 us
  between operations: 17.6 us -> 2.34 us
  other arithmetic: 41.5 us -> 26.6 us
    reduce_scatter x2 -> x0, waiting for transfers between devices: 288 us -> none  [local(): lax.psum_scatter(grad, 'dp', scatter_dimension=0, tiled=True)]
    ppermute x0 -> x40, waiting for transfers between devices: none -> 186 us  [the longest x32 186 us: exchange(): return lax.ppermute(array, ('section', 'dp'), pairs)]
    dot_general x60 -> x0, matrix products: 167 us -> none  [the longest x36 74.6 us: dot(): lax.dot_general(a, b, ((dims[0], dims[1]), ((), ())), preferred_element_t...]
    pallas_call x0 -> x13, Pallas kernels: none -> 163 us  [the longest x2 43.7 us: attention_backward(): call(functools.partial(attention_back_kernel, layer, heads), [smem()] + [...]
    ppermute x0 -> x40, starting transfers between devices: none -> 51.6 us  [the longest x32 32.2 us: exchange(): return lax.ppermute(array, ('section', 'dp'), pairs)]
    all_gather x1 -> x0, waiting for transfers between devices: 51.2 us -> none  [local(): whole = lax.all_gather(halves, 'dp', axis=0)]
    psum x1 -> x0, blocking collectives: 42 us -> none  [local(): tail = lax.psum(tail, 'dp')]
    reshape x7 -> x9, local copies, waits for them, and re-layouts: 42.2 us -> 1.59 us  [the longest x2 1.08 us: small_sums(): mixes = back.reshape(HEADS_ROWS, heads, width // heads).sum(axis=-1)]
  transfers between devices with their start and end apart: 38 -> 58, of which waited for: 9 -> 23; matrix products, arithmetic and copies ran while one was open for 30% -> 9% of each run, Pallas kernels for 0% -> 22%
where the time goes in v2:
time: 486 us; the launch traced here: 476 us
  waiting for transfers between devices  199 us (41%)
  Pallas kernels  163 us (34%)
  starting transfers between devices  56.1 us (12%)
  local copies, waits for them, and re-layouts  29.4 us (6%)
  other arithmetic  26.6 us (5%)
    ppermute x32, waiting for transfers between devices, exchange(): return lax.ppermute(array, ('section', 'dp'), pairs)  186 us
    pallas_call x2, Pallas kernels, attention_backward(): call(functools.partial(attention_back_kernel, layer, heads), [smem()] + [...  43.7 us
    pallas_call x2, Pallas kernels, attention_forward(): return run(meta, x, *rows, *own[:4], *other[:4])  38.8 us
    ppermute x32, starting transfers between devices, exchange(): return lax.ppermute(array, ('section', 'dp'), pairs)  32.2 us
    pallas_call x2, Pallas kernels, unpack(): pl.pallas_call(functools.partial(unpack_kernel, place), out_shape=outs, i...  24.2 us
    pallas_call x4, Pallas kernels, grad_blocks(): pl.pallas_call(kernel, out_shape=(out, out), grid_spec=pltpu.PrefetchScal...  22.7 us
    ppermute x8, starting transfers between devices, local(): hand = lambda array: lax.ppermute(array, 'section', [(1 - index, index)])  19.4 us
    unnamed x81, local copies, waits for them, and re-layouts  15.9 us
  transfers between devices with their start and end apart: 58, of which 23 were waited for; matrix products, arithmetic and copies ran while one was open for 9% of the time, Pallas kernels for 22%

profile of v2, /device:TPU:0, one launch (start us, length us, event | category | flops | bytes accessed | tf_op | source)
XLA Modules:
  0.0 476.1 jit_solution(8989796013390262106)
XLA Ops:
  17.8 19.3 %shard_map.228 = (bf16[256,1536]{1,0:T(8,128)(2,1)}, bf16[256,768]{1,0:T(8,128)(2,1)}, bf16[256,768]{1,0:T(8,128)(2,1)}, bf16[256,768]{1,0:T(8,128)(2,1)}, bf16[...) custom-call(s32[2]{0:T(128)} %pad_add_fusion.meta, bf16[256,768]{1,0:T(8,128)(2,1)} %dynamic-slice_bitcast_fusion.1.x, ...), custom_call_target="tpu_custom_call" | custom-call | flops 4831838208 | bytes 8650752 | tf_op jit(solution)/shard_map/pallas_call | solution.py:389
  37.1 10.5 %shard_map.229 = (bf16[256,768]{1,0:T(8,128)(2,1)}, bf16[256,2304]{1,0:T(8,128)(2,1)}, bf16[256,2304]{1,0:T(8,128)(2,1)}, bf16[256,3072]{1,0:T(8,128)(2,1)}, f32[8,768]{1,0:T(8,128)}) custom-call(s32[2]{0:T(128)} %pad_add_fusion.meta, f32[256,768]{1,0:T(8,128)} %get-tuple-element.71.residual, f32[32,768]{1,0:T(8,128)} %copy-done.27, f32[32,768]{1,0:T(8,128)} %copy-done.32, ...), custom_call_target="tpu_custom_call" | custom-call | flops 2415919104 | bytes 15728640 | tf_op jit(solution)/shard_map/pallas_call | solution.py:409
  47.6 19.5 %shard_map.230 = (bf16[256,1536]{1,0:T(8,128)(2,1)}, bf16[256,768]{1,0:T(8,128)(2,1)}, bf16[256,768]{1,0:T(8,128)(2,1)}, bf16[256,768]{1,0:T(8,128)(2,1)}, bf16[...) custom-call(s32[2]{0:T(128)} %pad_add_fusion.meta, bf16[256,768]{1,0:T(8,128)(2,1)} %get-tuple-element.74.x, ...), custom_call_target="tpu_custom_call" | custom-call | flops 4831838208 | bytes 8650752 | tf_op jit(solution)/shard_map/pallas_call | solution.py:389
  67.1 13.3 %shard_map.231 = (bf16[256,768]{1,0:T(8,128)(2,1)}, bf16[256,2304]{1,0:T(8,128)(2,1)}, bf16[256,2304]{1,0:T(8,128)(2,1)}, bf16[256,2304]{1,0:T(8,128)(2,1)}, bf1...) custom-call(s32[2]{0:T(128)} %pad_add_fusion.meta, f32[256,768]{1,0:T(8,128)} %get-tuple-element.75.residual, ...), custom_call_target="tpu_custom_call" | custom-call | flops 4831838208 | bytes 15728640 | tf_op jit(solution)/shard_map/pallas_call | solution.py:414
  87.9 6.3 %shard_map.232 = (bf16[1536,768]{1,0:T(8,128)(2,1)}, bf16[1536,768]{1,0:T(8,128)(2,1)}) custom-call(s32[1]{0:T(128)} %bitcast.9.shift_ref, bf16[256,2304]{1,0:T(8,128)(2,1)S(1)} %copy-done.11, bf16[256,2304]{1,0:T(8,128)(2,1)S(1)} %collective-permute-done.8.first2, bf16[256,2304]{1,0:T(8,128)(2,1)S(1)} %copy-done.12, ...), custom_call_target="tpu_custom_call" | custom-call | flops 2415919104 | bytes 4718592 | tf_op jit(solution)/shard_map/pallas_call | solution.py:539
  94.2 22.0 %shard_map.233 = (bf16[256,1536]{1,0:T(8,128)(2,1)}, bf16[256,1536]{1,0:T(8,128)(2,1)}, bf16[256,768]{1,0:T(8,128)(2,1)}, f32[32,768]{1,0:T(8,128)}) custom-call(s32[2]{0:T(128)} %pad_add_fusion.meta, bf16[256,768]{1,0:T(8,128)(2,1)} %get-tuple-element.74.x, f32[256,768]{1,0:T(8,128)} %get-tuple-element.84.resid_grad, ...), custom_call_target="tpu_custom_call" | custom-call | flops 7247757312 | bytes 9437184 | tf_op jit(solution)/shard_map/pallas_call | solution.py:448
  116.2 10.0 %shard_map.234 = (bf16[256,2304]{1,0:T(8,128)(2,1)}, bf16[256,2304]{1,0:T(8,128)(2,1)}, f32[256,768]{1,0:T(8,128)}, f32[8,768]{1,0:T(8,128)}) custom-call(s32[2]{0:T(128)} %pad_add_fusion.meta, f32[256,768]{1,0:T(8,128)} %get-tuple-element.71.residual, bf16[256,768]{1,0:T(8,128)(2,1)} %get-tuple-element.89.upstream, ...), custom_call_target="tpu_custom_call" | custom-call | flops 2415919104 | bytes 14155776 | tf_op jit(solution)/shard_map/pallas_call | solution.py:426
  137.7 3.6 shard_map.235
  141.3 7.6 %shard_map.236 = (bf16[1536,768]{1,0:T(8,128)(2,1)}, bf16[1536,768]{1,0:T(8,128)(2,1)}) custom-call(s32[1]{0:T(128)} %bitcast.9.shift_ref, bf16[256,2304]{1,0:T(8,128)(2,1)S(1)} %copy-done.10, bf16[256,2304]{1,0:T(8,128)(2,1)S(1)} %collective-permute-done.12.first2, bf16[256,2304]{1,0:T(8,128)(2,1)S(1)} %copy-done.13, ...), custom_call_target="tpu_custom_call" | custom-call | flops 2415919104 | bytes 4718592 | tf_op jit(solution)/shard_map/pallas_call | solution.py:539
  159.3 21.7 %shard_map.237 = (bf16[256,1536]{1,0:T(8,128)(2,1)}, bf16[256,1536]{1,0:T(8,128)(2,1)}, bf16[256,768]{1,0:T(8,128)(2,1)}, f32[32,768]{1,0:T(8,128)}) custom-call(s32[2]{0:T(128)} %pad_add_fusion.meta, bf16[256,768]{1,0:T(8,128)(2,1)} %dynamic-slice_bitcast_fusion.1.x, f32[256,768]{1,0:T(8,128)} %get-tuple-element.105.resid_grad, ...), custom_call_target="tpu_custom_call" | custom-call | flops 7247757312 | bytes 9437184 | tf_op jit(solution)/shard_map/pallas_call | solution.py:448
  181.4 3.7 add_convert_fusion.1
  186.6 3.6 add_convert_fusion.3
  195.4 5.1 %shard_map.238 = (bf16[1536,384]{1,0:T(8,128)(2,1)S(1)}, bf16[1536,384]{1,0:T(8,128)(2,1)S(1)}) custom-call(s32[1]{0:T(128)} %bitcast.10.shift_ref, bf16[256,1536]{1,0:T(8,128)(2,1)} %get-tuple-element.111.both, bf16[256,1536]{1,0:T(8,128)(2,1)S(1)} %collective-permute-done.15.both2, bf16[256,1536]{1,0:T(8,128)(2,1)S(1)} %copy-done.20, ...), custom_call_target="tpu_custom_call" | custom-call | flops 1207959552 | bytes 2359296 | tf_op jit(solution)/shard_map/pallas_call | solution.py:539
  204.0 10.3 %collective-permute-done.36 = bf16[768,768]{1,0:T(8,128)(2,1)} collective-permute-done((bf16[768,768]{1,0:T(8,128)(2,1)}, bf16[768,768]{1,0:T(8,128)(2,1)}, u32[]{:S(2)}, u32[]{:S(2)}) %collective-permute-start.36) | collective-permute-done | bytes 1179680 | tf_op jit(solution)/shard_map/ppermute | solution.py:481
  218.3 39.7 %collective-permute-done.46 = bf16[384,768]{1,0:T(8,128)(2,1)S(1)} collective-permute-done((bf16[384,768]{1,0:T(8,128)(2,1)S(1)}, bf16[384,768]{1,0:T(8,128)(2,1)S(1)}, u32[]{:S(2)}, u32[]{:S(2)}) %collective-permute-start.46) | collective-permute-done | bytes 589856 | tf_op jit(solution)/shard_map/ppermute | solution.py:481
  259.9 7.4 %collective-permute-done.37 = bf16[384,768]{1,0:T(8,128)(2,1)S(1)} collective-permute-done((bf16[384,768]{1,0:T(8,128)(2,1)S(1)}, bf16[384,768]{1,0:T(8,128)(2,1)S(1)}, u32[]{:S(2)}, u32[]{:S(2)}) %collective-permute-start.37) | collective-permute-done | bytes 589856 | tf_op jit(solution)/shard_map/ppermute | solution.py:481
  273.6 17.8 %collective-permute-done.47 = bf16[384,768]{1,0:T(8,128)(2,1)S(1)} collective-permute-done((bf16[384,768]{1,0:T(8,128)(2,1)S(1)}, bf16[384,768]{1,0:T(8,128)(2,1)S(1)}, u32[]{:S(2)}, u32[]{:S(2)}) %collective-permute-start.47) | collective-permute-done | bytes 589856 | tf_op jit(solution)/shard_map/ppermute | solution.py:481
  291.7 7.0 %collective-permute-done.38 = bf16[384,768]{1,0:T(8,128)(2,1)S(1)} collective-permute-done((bf16[384,768]{1,0:T(8,128)(2,1)S(1)}, bf16[384,768]{1,0:T(8,128)(2,1)S(1)}, u32[]{:S(2)}, u32[]{:S(2)}) %collective-permute-start.38) | collective-permute-done | bytes 589856 | tf_op jit(solution)/shard_map/ppermute | solution.py:481
  298.9 5.2 %collective-permute-done.29 = bf16[384,384]{1,0:T(8,128)(2,1)S(1)} collective-permute-done((bf16[384,384]{1,0:T(8,128)(2,1)S(1)}, bf16[384,384]{1,0:T(8,128)(2,1)S(1)}, u32[]{:S(2)}, u32[]{:S(2)}) %collective-permute-start.29) | collective-permute-done | bytes 294944 | tf_op jit(solution)/shard_map/ppermute | solution.py:481
  306.4 10.3 %collective-permute-done.48 = bf16[384,768]{1,0:T(8,128)(2,1)S(1)} collective-permute-done((bf16[384,768]{1,0:T(8,128)(2,1)S(1)}, bf16[384,768]{1,0:T(8,128)(2,1)S(1)}, u32[]{:S(2)}, u32[]{:S(2)}) %collective-permute-start.48) | collective-permute-done | bytes 589856 | tf_op jit(solution)/shard_map/ppermute | solution.py:481
  319.0 10.3 %collective-permute-done.39 = bf16[384,768]{1,0:T(8,128)(2,1)S(1)} collective-permute-done((bf16[384,768]{1,0:T(8,128)(2,1)S(1)}, bf16[384,768]{1,0:T(8,128)(2,1)S(1)}, u32[]{:S(2)}, u32[]{:S(2)}) %collective-permute-start.39) | collective-permute-done | bytes 589856 | tf_op jit(solution)/shard_map/ppermute | solution.py:481
  332.8 8.9 %collective-permute-done.20 = bf16[384,384]{1,0:T(8,128)(2,1)S(1)} collective-permute-done((bf16[384,384]{1,0:T(8,128)(2,1)S(1)}, bf16[384,384]{1,0:T(8,128)(2,1)S(1)}, u32[]{:S(2)}, u32[]{:S(2)}) %collective-permute-start.20) | collective-permute-done | bytes 294944 | tf_op jit(solution)/shard_map/ppermute | solution.py:481
  344.0 18.1 %collective-permute-done.40 = bf16[768,768]{1,0:T(8,128)(2,1)S(1)} collective-permute-done((bf16[768,768]{1,0:T(8,128)(2,1)S(1)}, bf16[768,768]{1,0:T(8,128)(2,1)S(1)}, u32[]{:S(2)}, u32[]{:S(2)}) %collective-permute-start.40) | collective-permute-done | bytes 1179680 | tf_op jit(solution)/shard_map/ppermute | solution.py:481
  365.1 3.7 collective-permute-done.21
  368.9 3.7 collective-permute-done.56
  374.0 4.6 collective-permute-done.57
  378.5 30.8 %collective-permute-done.22 = bf16[768,384]{1,0:T(8,128)(2,1)S(1)} collective-permute-done((bf16[768,384]{1,0:T(8,128)(2,1)S(1)}, bf16[768,384]{1,0:T(8,128)(2,1)S(1)}, u32[]{:S(2)}, u32[]{:S(2)}) %collective-permute-start.22) | collective-permute-done | bytes 589856 | tf_op jit(solution)/shard_map/ppermute | solution.py:481
  417.7 5.4 %collective-permute-start.51 = (bf16[1536,768]{1,0:T(8,128)(2,1)S(1)}, bf16[1536,768]{1,0:T(8,128)(2,1)}, u32[]{:S(2)}, u32[]{:S(2)}) collective-permute-start(bf16[1536,768]{1,0:T(8,128)(2,1)S(1)} %pad_maximum_fusion.1.refs_4_), channel_id=1, source_target_pairs={{0,16},{1,17},{2,18},{3,19},{4,20},{5,21},{6,22},{7,23},{8,24},{9,... | collective-permute-start | bytes 7077896 | tf_op jit(solution)/shard_map/ppermute | solution.py:741
  423.1 7.7 %collective-permute-done.23.refs_1_ = bf16[1536,384]{1,0:T(8,128)(2,1)} collective-permute-done((bf16[1536,384]{1,0:T(8,128)(2,1)}, bf16[1536,384]{1,0:T(8,128)(2,1)}, u32[]{:S(2)}, u32[]{:S(2)}) %collective-permute-start.23) | collective-permute-done | bytes 1179680 | tf_op jit(solution)/shard_map/ppermute | solution.py:481
  432.2 5.9 %collective-permute-start.52 = (bf16[1536,768]{1,0:T(8,128)(2,1)}, bf16[1536,768]{1,0:T(8,128)(2,1)}, u32[]{:S(2)}, u32[]{:S(2)}) collective-permute-start(bf16[1536,768]{1,0:T(8,128)(2,1)} %collective-permute-done.50.refs_5_), channel_id=1, source_target_pairs={{0,16},{1,17},{2,18},{3,19},{4,20},{5,21},{6,22},{7,23},{8,24},{9,... | collective-permute-start | bytes 7077896 | tf_op jit(solution)/shard_map/ppermute | solution.py:741
  451.6 10.5 %shard_map.239 = (f32[1,768,768]{2,1,0:T(8,128)}, f32[1,768,768]{2,1,0:T(8,128)}, f32[1,768,768]{2,1,0:T(8,128)}, f32[1,768,768]{2,1,0:T(8,128)}) custom-call(s32[3]{0:T(128)S(1)} %pad_add_fusion.1.meta, bf16[1536,384]{1,0:T(8,128)(2,1)} %pad_maximum_fusion.2.refs_0_, bf16[1536,384]{1,0:T(8,128)(2,1)} %collective-permute-done.23.refs_1_, ...), custom_call_target="tpu_custom_call" | custom-call | bytes 14155776 | tf_op jit(solution)/shard_map/pallas_call | solution.py:653
  462.2 13.6 %shard_map.240 = (f32[1,768,3072]{2,1,0:T(8,128)}, f32[1,3072,768]{2,1,0:T(8,128)}) custom-call(s32[3]{0:T(128)S(1)} %pad_add_fusion.2.meta, bf16[1536,768]{1,0:T(8,128)(2,1)} %pad_maximum_fusion.refs_0_, bf16[1536,768]{1,0:T(8,128)(2,1)} %collective-permute-done.41.refs_1_, bf16[1536,768]{1,0:T(8,128)(2,1)} %collective-permute-done.42.refs_2_, ...), custom_call_target="tpu_custom_call" | custom-call | bytes 28311552 | tf_op jit(solution)/shard_map/pallas_call | solution.py:653
  (258 shorter events, 106.6 us)
Async XLA Ops:
  8.9 28.1 %collective-permute-start.5 = (bf16[1,768,3072]{2,1,0:T(8,128)(2,1)}, bf16[1,768,3072]{2,1,0:T(8,128)(2,1)}, u32[]{:S(2)}, u32[]{:S(2)}) collective-permute-start(bf16[1,768,3072]{2,1,0:T(8,128)(2,1)} %w_in.5), channel_id=1, source_target_pairs={{0,16},{16,0},{1,17},{17,1},{2,18},{18,2},{3,19},{19,3},{4,20},{20... | collective-permute-start | bytes 14155784 | tf_op jit(solution)/shard_map/ppermute | solution.py:689
  10.0 27.1 %collective-permute-start.6 = (bf16[1,3072,768]{2,1,0:T(8,128)(2,1)}, bf16[1,3072,768]{2,1,0:T(8,128)(2,1)}, u32[]{:S(2)}, u32[]{:S(2)}) collective-permute-start(bf16[1,3072,768]{2,1,0:T(8,128)(2,1)} %w_out.5), channel_id=1, source_target_pairs={{0,16},{16,0},{1,17},{17,1},{2,18},{18,2},{3,19},{19,3},{4,20},{20... | collective-permute-start | bytes 14155784 | tf_op jit(solution)/shard_map/ppermute | solution.py:689
  81.0 60.2 %collective-permute-start.12 = (bf16[256,2304]{1,0:T(8,128)(2,1)}, bf16[256,2304]{1,0:T(8,128)(2,1)S(1)}, u32[]{:S(2)}, u32[]{:S(2)}) collective-permute-start(bf16[256,2304]{1,0:T(8,128)(2,1)} %get-tuple-element.100), channel_id=1, source_target_pairs={{0,16},{16,0},{1,17},{17,1},{2,18},{18,2},{3,19},{19,3},{4,20},{20... | collective-permute-start | bytes 3538952 | tf_op jit(solution)/shard_map/ppermute | solution.py:689
  127.2 54.2 %collective-permute-start.44 = (bf16[1536,768]{1,0:T(8,128)(2,1)}, bf16[1536,768]{1,0:T(8,128)(2,1)}, u32[]{:S(2)}, u32[]{:S(2)}) collective-permute-start(bf16[1536,768]{1,0:T(8,128)(2,1)} %get-tuple-element.82), channel_id=1, source_target_pairs={{0,1},{1,0},{2,3},{3,2},{4,5},{5,4},{6,7},{7,6},{8,9},{9,8},{10,11... | collective-permute-start | bytes 7077896 | tf_op jit(solution)/shard_map/ppermute | solution.py:481
  148.9 37.7 %collective-permute-start.35 = (bf16[1536,768]{1,0:T(8,128)(2,1)}, bf16[1536,768]{1,0:T(8,128)(2,1)}, u32[]{:S(2)}, u32[]{:S(2)}) collective-permute-start(bf16[1536,768]{1,0:T(8,128)(2,1)} %get-tuple-element.103), channel_id=1, source_target_pairs={{0,1},{1,0},{2,3},{3,2},{4,5},{5,4},{6,7},{7,6},{8,9},{9,8},{10,11... | collective-permute-start | bytes 7077896 | tf_op jit(solution)/shard_map/ppermute | solution.py:481
  153.1 41.0 %collective-permute-start.15 = (bf16[256,1536]{1,0:T(8,128)(2,1)}, bf16[256,1536]{1,0:T(8,128)(2,1)S(1)}, u32[]{:S(2)}, u32[]{:S(2)}) collective-permute-start(bf16[256,1536]{1,0:T(8,128)(2,1)} %get-tuple-element.111.both), channel_id=1, source_target_pairs={{0,16},{16,0},{1,17},{17,1},{2,18},{18,2},{3,19},{19,3},{4,20},{20... | collective-permute-start | bytes 2359304 | tf_op jit(solution)/shard_map/ppermute | solution.py:689
  157.7 34.7 %collective-permute-start.26 = (bf16[1536,384]{1,0:T(8,128)(2,1)S(1)}, bf16[1536,384]{1,0:T(8,128)(2,1)}, u32[]{:S(2)}, u32[]{:S(2)}) collective-permute-start(bf16[1536,384]{1,0:T(8,128)(2,1)S(1)} %get-tuple-element.97), channel_id=1, source_target_pairs={{0,4},{1,5},{2,6},{3,7},{4,0},{5,1},{6,2},{7,3},{8,12},{9,13},{10,... | collective-permute-start | bytes 3538952 | tf_op jit(solution)/shard_map/ppermute | solution.py:481
  200.6 71.2 %collective-permute-start.17 = (bf16[1536,384]{1,0:T(8,128)(2,1)S(1)}, bf16[1536,384]{1,0:T(8,128)(2,1)S(1)}, u32[]{:S(2)}, u32[]{:S(2)}) collective-permute-start(bf16[1536,384]{1,0:T(8,128)(2,1)S(1)} %get-tuple-element.115), channel_id=1, source_target_pairs={{0,4},{1,5},{2,6},{3,7},{4,0},{5,1},{6,2},{7,3},{8,12},{9,13},{10,... | collective-permute-start | bytes 3538952 | tf_op jit(solution)/shard_map/ppermute | solution.py:481
  202.9 55.1 %collective-permute-start.46 = (bf16[384,768]{1,0:T(8,128)(2,1)S(1)}, bf16[384,768]{1,0:T(8,128)(2,1)S(1)}, u32[]{:S(2)}, u32[]{:S(2)}) collective-permute-start(bf16[384,768]{1,0:T(8,128)(2,1)S(1)} %add_convert_fusion.6), channel_id=1, source_target_pairs={{0,4},{1,5},{2,6},{3,7},{4,0},{5,1},{6,2},{7,3},{8,12},{9,13},{10,... | collective-permute-start | bytes 1769480 | tf_op jit(solution)/shard_map/ppermute | solution.py:481
  215.5 51.8 %collective-permute-start.37 = (bf16[384,768]{1,0:T(8,128)(2,1)S(1)}, bf16[384,768]{1,0:T(8,128)(2,1)S(1)}, u32[]{:S(2)}, u32[]{:S(2)}) collective-permute-start(bf16[384,768]{1,0:T(8,128)(2,1)S(1)} %add_convert_fusion.10), channel_id=1, source_target_pairs={{0,4},{1,5},{2,6},{3,7},{4,0},{5,1},{6,2},{7,3},{8,12},{9,13},{10,... | collective-permute-start | bytes 1769480 | tf_op jit(solution)/shard_map/ppermute | solution.py:481
  216.0 115.2 %collective-permute-start.54 = (f32[32,128]{1,0:T(8,128)S(1)}, f32[32,128]{1,0:T(8,128)S(1)}, u32[]{:S(2)}, u32[]{:S(2)}) collective-permute-start(f32[32,128]{1,0:T(8,128)S(1)} %fusion.2), channel_id=1, source_target_pairs={{0,1},{1,0},{2,3},{3,2},{4,5},{5,4},{6,7},{7,6},{8,9},{9,8},{10,11... | collective-permute-start | bytes 49160 | tf_op jit(solution)/shard_map/ppermute | solution.py:481
  217.4 51.7 %collective-permute-start.28 = (bf16[384,384]{1,0:T(8,128)(2,1)S(1)}, bf16[384,384]{1,0:T(8,128)(2,1)S(1)}, u32[]{:S(2)}, u32[]{:S(2)}) collective-permute-start(bf16[384,384]{1,0:T(8,128)(2,1)S(1)} %add_convert_fusion.18), channel_id=1, source_target_pairs={{0,2},{1,3},{2,0},{3,1},{4,6},{5,7},{6,4},{7,5},{8,10},{9,11},{10,... | collective-permute-start | bytes 884744 | tf_op jit(solution)/shard_map/ppermute | solution.py:481
  259.3 32.1 %collective-permute-start.47 = (bf16[384,768]{1,0:T(8,128)(2,1)S(1)}, bf16[384,768]{1,0:T(8,128)(2,1)S(1)}, u32[]{:S(2)}, u32[]{:S(2)}) collective-permute-start(bf16[384,768]{1,0:T(8,128)(2,1)S(1)} %add_convert_fusion.5), channel_id=1, source_target_pairs={{0,8},{1,9},{2,10},{3,11},{4,12},{5,13},{6,14},{7,15},{8,0},{9,1},... | collective-permute-start | bytes 1769480 | tf_op jit(solution)/shard_map/ppermute | solution.py:481
  268.6 30.1 %collective-permute-start.38 = (bf16[384,768]{1,0:T(8,128)(2,1)S(1)}, bf16[384,768]{1,0:T(8,128)(2,1)S(1)}, u32[]{:S(2)}, u32[]{:S(2)}) collective-permute-start(bf16[384,768]{1,0:T(8,128)(2,1)S(1)} %add_convert_fusion.9), channel_id=1, source_target_pairs={{0,8},{1,9},{2,10},{3,11},{4,12},{5,13},{6,14},{7,15},{8,0},{9,1},... | collective-permute-start | bytes 1769480 | tf_op jit(solution)/shard_map/ppermute | solution.py:481
  269.3 34.8 %collective-permute-start.29 = (bf16[384,384]{1,0:T(8,128)(2,1)S(1)}, bf16[384,384]{1,0:T(8,128)(2,1)S(1)}, u32[]{:S(2)}, u32[]{:S(2)}) collective-permute-start(bf16[384,384]{1,0:T(8,128)(2,1)S(1)} %add_convert_fusion.17), channel_id=1, source_target_pairs={{0,8},{1,9},{2,10},{3,11},{4,12},{5,13},{6,14},{7,15},{8,0},{9,1},... | collective-permute-start | bytes 884744 | tf_op jit(solution)/shard_map/ppermute | solution.py:481
  272.1 33.7 %collective-permute-start.18 = (bf16[768,384]{1,0:T(8,128)(2,1)S(1)}, bf16[768,384]{1,0:T(8,128)(2,1)S(1)}, u32[]{:S(2)}, u32[]{:S(2)}) collective-permute-start(bf16[768,384]{1,0:T(8,128)(2,1)S(1)} %get-tuple-element.188), channel_id=1, source_target_pairs={{0,1},{1,0},{2,3},{3,2},{4,5},{5,4},{6,7},{7,6},{8,9},{9,8},{10,11... | collective-permute-start | bytes 1769480 | tf_op jit(solution)/shard_map/ppermute | solution.py:481
  291.6 25.1 %collective-permute-start.48 = (bf16[384,768]{1,0:T(8,128)(2,1)S(1)}, bf16[384,768]{1,0:T(8,128)(2,1)S(1)}, u32[]{:S(2)}, u32[]{:S(2)}) collective-permute-start(bf16[384,768]{1,0:T(8,128)(2,1)S(1)} %add_convert_fusion.4), channel_id=1, source_target_pairs={{0,4},{1,5},{2,6},{3,7},{4,0},{5,1},{6,2},{7,3},{8,12},{9,13},{10,... | collective-permute-start | bytes 1769480 | tf_op jit(solution)/shard_map/ppermute | solution.py:481
  298.8 30.5 %collective-permute-start.39 = (bf16[384,768]{1,0:T(8,128)(2,1)S(1)}, bf16[384,768]{1,0:T(8,128)(2,1)S(1)}, u32[]{:S(2)}, u32[]{:S(2)}) collective-permute-start(bf16[384,768]{1,0:T(8,128)(2,1)S(1)} %add_convert_fusion.8), channel_id=1, source_target_pairs={{0,4},{1,5},{2,6},{3,7},{4,0},{5,1},{6,2},{7,3},{8,12},{9,13},{10,... | collective-permute-start | bytes 1769480 | tf_op jit(solution)/shard_map/ppermute | solution.py:481
  305.8 25.2 %collective-permute-start.19 = (bf16[384,384]{1,0:T(8,128)(2,1)S(1)}, bf16[384,384]{1,0:T(8,128)(2,1)S(1)}, u32[]{:S(2)}, u32[]{:S(2)}) collective-permute-start(bf16[384,384]{1,0:T(8,128)(2,1)S(1)} %add_convert_fusion.22), channel_id=1, source_target_pairs={{0,2},{1,3},{2,0},{3,1},{4,6},{5,7},{6,4},{7,5},{8,10},{9,11},{10,... | collective-permute-start | bytes 884744 | tf_op jit(solution)/shard_map/ppermute | solution.py:481
  316.8 25.5 %collective-permute-start.49 = (bf16[768,768]{1,0:T(8,128)(2,1)S(1)}, bf16[768,768]{1,0:T(8,128)(2,1)S(1)}, u32[]{:S(2)}, u32[]{:S(2)}) collective-permute-start(bf16[768,768]{1,0:T(8,128)(2,1)S(1)} %pad_maximum_fusion.5), channel_id=1, source_target_pairs={{0,2},{1,3},{2,0},{3,1},{4,6},{5,7},{6,4},{7,5},{8,10},{9,11},{10,... | collective-permute-start | bytes 3538952 | tf_op jit(solution)/shard_map/ppermute | solution.py:481
  329.4 32.7 %collective-permute-start.40 = (bf16[768,768]{1,0:T(8,128)(2,1)S(1)}, bf16[768,768]{1,0:T(8,128)(2,1)S(1)}, u32[]{:S(2)}, u32[]{:S(2)}) collective-permute-start(bf16[768,768]{1,0:T(8,128)(2,1)S(1)} %pad_maximum_fusion.4), channel_id=1, source_target_pairs={{0,2},{1,3},{2,0},{3,1},{4,6},{5,7},{6,4},{7,5},{8,10},{9,11},{10,... | collective-permute-start | bytes 3538952 | tf_op jit(solution)/shard_map/ppermute | solution.py:481
  331.2 33.8 %collective-permute-start.55 = (f32[32,128]{1,0:T(8,128)S(1)}, f32[32,128]{1,0:T(8,128)S(1)}, u32[]{:S(2)}, u32[]{:S(2)}) collective-permute-start(f32[32,128]{1,0:T(8,128)S(1)} %fusion.7), channel_id=1, source_target_pairs={{0,2},{1,3},{2,0},{3,1},{4,6},{5,7},{6,4},{7,5},{8,10},{9,11},{10,... | collective-permute-start | bytes 49160 | tf_op jit(solution)/shard_map/ppermute | solution.py:481
  332.0 79.8 %collective-permute-start.32 = (bf16[1536,384]{1,0:T(8,128)(2,1)S(1)}, bf16[1536,384]{1,0:T(8,128)(2,1)S(1)}, u32[]{:S(2)}, u32[]{:S(2)}) collective-permute-start(bf16[1536,384]{1,0:T(8,128)(2,1)S(1)} %pad_maximum_fusion.3.refs_4_), channel_id=1, source_target_pairs={{0,4},{1,5},{2,6},{3,7},{4,0},{5,1},{6,2},{7,3},{8,12},{9,13},{10,... | collective-permute-start | bytes 3538952 | tf_op jit(solution)/shard_map/ppermute | solution.py:481
  341.7 27.1 %collective-permute-start.21 = (bf16[384,384]{1,0:T(8,128)(2,1)S(1)}, bf16[384,384]{1,0:T(8,128)(2,1)S(1)}, u32[]{:S(2)}, u32[]{:S(2)}) collective-permute-start(bf16[384,384]{1,0:T(8,128)(2,1)S(1)} %add_convert_fusion.20), channel_id=1, source_target_pairs={{0,2},{1,3},{2,0},{3,1},{4,6},{5,7},{6,4},{7,5},{8,10},{9,11},{10,... | collective-permute-start | bytes 884744 | tf_op jit(solution)/shard_map/ppermute | solution.py:481
  342.4 89.7 %collective-permute-start.50 = (bf16[1536,768]{1,0:T(8,128)(2,1)S(1)}, bf16[1536,768]{1,0:T(8,128)(2,1)}, u32[]{:S(2)}, u32[]{:S(2)}) collective-permute-start(bf16[1536,768]{1,0:T(8,128)(2,1)S(1)} %pad_maximum_fusion.1.refs_4_), channel_id=1, source_target_pairs={{0,1},{1,0},{2,3},{3,2},{4,5},{5,4},{6,7},{7,6},{8,9},{9,8},{10,11... | collective-permute-start | bytes 7077896 | tf_op jit(solution)/shard_map/ppermute | solution.py:481
  363.6 74.5 %collective-permute-start.41 = (bf16[1536,768]{1,0:T(8,128)(2,1)}, bf16[1536,768]{1,0:T(8,128)(2,1)}, u32[]{:S(2)}, u32[]{:S(2)}) collective-permute-start(bf16[1536,768]{1,0:T(8,128)(2,1)} %pad_maximum_fusion.refs_0_), channel_id=1, source_target_pairs={{0,1},{1,0},{2,3},{3,2},{4,5},{5,4},{6,7},{7,6},{8,9},{9,8},{10,11... | collective-permute-start | bytes 7077896 | tf_op jit(solution)/shard_map/ppermute | solution.py:481
  372.5 36.8 %collective-permute-start.22 = (bf16[768,384]{1,0:T(8,128)(2,1)S(1)}, bf16[768,384]{1,0:T(8,128)(2,1)S(1)}, u32[]{:S(2)}, u32[]{:S(2)}) collective-permute-start(bf16[768,384]{1,0:T(8,128)(2,1)S(1)} %pad_maximum_fusion.6), channel_id=1, source_target_pairs={{0,1},{1,0},{2,3},{3,2},{4,5},{5,4},{6,7},{7,6},{8,9},{9,8},{10,11... | collective-permute-start | bytes 1769480 | tf_op jit(solution)/shard_map/ppermute | solution.py:481
  378.5 35.9 %collective-permute-start.14 = (bf16[256,768]{1,0:T(8,128)(2,1)S(1)}, bf16[256,768]{1,0:T(8,128)(2,1)}, u32[]{:S(2)}, u32[]{:S(2)}) collective-permute-start(bf16[256,768]{1,0:T(8,128)(2,1)S(1)} %broadcast_select_fusion), channel_id=1, source_target_pairs={{0,16},{16,0},{1,17},{17,1},{2,18},{18,2},{3,19},{19,3},{4,20},{20... | collective-permute-start | bytes 1179656 | tf_op jit(solution)/shard_map/ppermute | solution.py:689
  415.4 26.2 %collective-permute-start.24 = (bf16[1536,384]{1,0:T(8,128)(2,1)}, bf16[1536,384]{1,0:T(8,128)(2,1)}, u32[]{:S(2)}, u32[]{:S(2)}) collective-permute-start(bf16[1536,384]{1,0:T(8,128)(2,1)} %pad_maximum_fusion.2.refs_0_), channel_id=1, source_target_pairs={{16,0},{17,1},{18,2},{19,3},{20,4},{21,5},{22,6},{23,7},{24,8},{25... | collective-permute-start | bytes 3538952 | tf_op jit(solution)/shard_map/ppermute | solution.py:741
  417.7 44.4 %collective-permute-start.51 = (bf16[1536,768]{1,0:T(8,128)(2,1)S(1)}, bf16[1536,768]{1,0:T(8,128)(2,1)}, u32[]{:S(2)}, u32[]{:S(2)}) collective-permute-start(bf16[1536,768]{1,0:T(8,128)(2,1)S(1)} %pad_maximum_fusion.1.refs_4_), channel_id=1, source_target_pairs={{0,16},{1,17},{2,18},{3,19},{4,20},{5,21},{6,22},{7,23},{8,24},{9,... | collective-permute-start | bytes 7077896 | tf_op jit(solution)/shard_map/ppermute | solution.py:741
  430.9 31.3 %collective-permute-start.42 = (bf16[1536,768]{1,0:T(8,128)(2,1)}, bf16[1536,768]{1,0:T(8,128)(2,1)}, u32[]{:S(2)}, u32[]{:S(2)}) collective-permute-start(bf16[1536,768]{1,0:T(8,128)(2,1)} %pad_maximum_fusion.refs_0_), channel_id=1, source_target_pairs={{16,0},{17,1},{18,2},{19,3},{20,4},{21,5},{22,6},{23,7},{24,8},{25... | collective-permute-start | bytes 7077896 | tf_op jit(solution)/shard_map/ppermute | solution.py:741
  432.2 30.0 %collective-permute-start.52 = (bf16[1536,768]{1,0:T(8,128)(2,1)}, bf16[1536,768]{1,0:T(8,128)(2,1)}, u32[]{:S(2)}, u32[]{:S(2)}) collective-permute-start(bf16[1536,768]{1,0:T(8,128)(2,1)} %collective-permute-done.50.refs_5_), channel_id=1, source_target_pairs={{0,16},{1,17},{2,18},{3,19},{4,20},{5,21},{6,22},{7,23},{8,24},{9,... | collective-permute-start | bytes 7077896 | tf_op jit(solution)/shard_map/ppermute | solution.py:741
  (66 other events, 639.6 us)
